TPU v7x, 128 devices: a whole 4x4x4 slice. The times are simulated.
128 devices in a mesh: mesh: 32 (over z, y_hi, x), freq: 4 (over y_lo, core).
Axes of the slice: x: 4, y: 4 (y_hi: 2, y_lo: 2; y = y_hi * 2 + y_lo), z: 4, core: 2. Of those that a mesh axis runs over, the one named last changes fastest.
Arguments:
- spectra: float32 [36, 36, 16384], P('freq', None, 'mesh'), may hold values from 0.1 to 2
- coords: float32 [2, 16384], P(None, 'mesh'), may hold values from -5 to 5
- inv_area: float32 [16384], P('mesh'), may hold values from 0.3 to 1
- wind_vector: float32 [2, 16384], P(None, 'mesh'), may hold values from -6 to 6
- neighbours: int32 [8, 16384], P(None, 'mesh'), may hold values from 0 to 767, as said below
- send_nodes: int32 [1024, 8], P('mesh'), may hold values from 0 to 511
- send_count: int32 [1024], P('mesh'), may hold values from 1 to 8, as said below
Outputs:
- updated: float32 [36, 36, 16384], P('freq', None, 'mesh')
Inputs may be any that keep to these rules, and one draw needn't show every extreme that they name: `neighbours`: an entry below 512 is a node of the same partition; an entry 512 + q * 8 + c names slot c of the list that partition q sends to this partition, with c below that list's count; slots past a node's degree name the node itself; some node uses all 8 slots. `send_count`: in every draw some partition receives exactly 8 nodes from every partition.
All inputs are finite; a program needn't handle non-finite values.
Results may differ from a plain program's by a relative error of at most 0.00002.
Values sent between devices are 32-bit elements; how exact they have to be, the bound alone decides.
No kernel may reach another device: no remote copies, remote signals or barrier semaphores. Data moves between devices by JAX's collectives and lax.ppermute only.
A program may use at most 64 MiB of HBM per device.

v0:
```python
import math

import jax
import jax.numpy as jnp
import numpy as np
from jax import lax
from jax.experimental import pallas as pl
from jax.experimental.pallas import tpu as pltpu
from jax.sharding import PartitionSpec as P

NF = 36
ND = 36
K = 8
NP = 512
CAP = 8
N_MESH = 32
GHOSTS = N_MESH * CAP
BAND = 9
UP_REACH = 2
DOWN_REACH = 3
UP_SHIFT = 1
DOWN_SHIFT = 3
STRIDE = 40
ROWS = BAND * STRIDE + 8
LANES = 384

time_step = 0.5
group_scale = 0.8
quad_coupling = 0.25
wind_growth = 0.1
RATIOS = np.power(np.float64(1.1), np.arange(NF) - NF // 2)


def bf16_pieces(x):
    high = x.astype(jnp.bfloat16)
    low = (x - high.astype(jnp.float32)).astype(jnp.bfloat16)
    return jnp.concatenate([high, low], axis=0)


def exact_rows(c):
    high = c.astype(jnp.bfloat16).astype(jnp.float32)
    mid = (c - high).astype(jnp.bfloat16).astype(jnp.float32)
    return high + mid, (c - high) - mid


def by_band(band, values):
    picked = jnp.float32(values[3])
    for index in (2, 1, 0):
        picked = jnp.where(band == index, jnp.float32(values[index]), picked)
    return picked


def ratio_of(band, f):
    return by_band(band, [RATIOS[b * BAND + f] for b in range(NF // BAND)])


def scale_of(band, f):
    return by_band(band, [time_step * group_scale / RATIOS[b * BAND + f] for b in range(NF // BAND)])


def one_hot(entry_row, first, count):
    node = lax.broadcasted_iota(jnp.int32, (count, entry_row.shape[1]), 0) + first
    return jnp.where(node == entry_row, 1.0, 0.0).astype(jnp.bfloat16)


def gather(pieces, entry_row, first):
    got = jnp.dot(pieces, one_hot(entry_row, first, pieces.shape[1]), preferred_element_type=jnp.float32)
    return got[:ROWS] + got[ROWS:]


def fill_rows(rows_ref, planes, coords):
    rows_ref[...] = jnp.zeros_like(rows_ref)
    for f in range(BAND):
        rows_ref[f * STRIDE : f * STRIDE + ND, :] = planes[f]
    if coords is not None:
        base = BAND * STRIDE
        for axis in range(2):
            first, second = exact_rows(coords[axis : axis + 1, :])
            rows_ref[base + 2 * axis : base + 2 * axis + 1, :] = first
            rows_ref[base + 2 * axis + 1 : base + 2 * axis + 2, :] = second


def pack(pieces, send_ref, count_ref):
    slots = jnp.concatenate([send_ref[...].astype(jnp.float32)] * N_MESH, axis=0)
    counts = jnp.broadcast_to(count_ref[...].astype(jnp.float32), slots.shape)
    row = lax.broadcasted_iota(jnp.int32, slots.shape, 0)
    mine = lax.broadcasted_iota(jnp.int32, slots.shape, 1) == row // CAP
    node = jnp.sum(jnp.where(mine, slots, 0.0), axis=1, keepdims=True)
    count = jnp.sum(jnp.where(mine, counts, 0.0), axis=1, keepdims=True)
    place = lax.broadcasted_iota(jnp.int32, (GHOSTS, 1), 0) % CAP
    node = jnp.where(place.astype(jnp.float32) < count, node, -1.0).astype(jnp.int32)
    hot = jnp.where(lax.broadcasted_iota(jnp.int32, (GHOSTS, NP), 1) == node, 1.0, 0.0).astype(jnp.bfloat16)
    dims = (((1,), (1,)), ((), ()))
    return lax.dot_general(hot, pieces[:ROWS], dims, preferred_element_type=jnp.float32) + lax.dot_general(
        hot, pieces[ROWS:], dims, preferred_element_type=jnp.float32
    )


def wide(table):
    return jnp.concatenate([table] * (NP // 128), axis=1)


def pack_kernel(spectra_ref, coords_ref, send_ref, count_ref, out_ref, rows_ref):
    fill_rows(rows_ref, [spectra_ref[f] for f in range(BAND)], coords_ref[...])
    out_ref[:, :ROWS] = pack(bf16_pieces(rows_ref[...]), send_ref, count_ref)
    out_ref[:, ROWS:] = jnp.zeros((GHOSTS, LANES - ROWS), jnp.float32)


def facing(cosine, sine, coords, got):
    base = BAND * STRIDE
    delta_x = (got[base : base + 1] + got[base + 1 : base + 2]) - coords[0:1]
    delta_y = (got[base + 2 : base + 3] + got[base + 3 : base + 4]) - coords[1:2]
    return jnp.maximum(-(cosine * delta_x + sine * delta_y), 0.0)


def rolled(x, shift):
    shift = shift % ND
    return jnp.concatenate([x[ND - shift :], x[: ND - shift]], axis=0)


def local_kernel(
    band_ref, spectra_ref, lower_ref, upper_ref, coords_ref, wind_ref, near_ref, table_ref,
    base_ref, partial_ref, inflow_ref, rows_ref,
):
    band = band_ref[0]
    coords = coords_ref[...]
    fill_rows(rows_ref, [spectra_ref[f] for f in range(BAND)], coords)
    pieces = bf16_pieces(rows_ref[...])
    cosine, sine = wide(table_ref[0])[:ND], wide(table_ref[1])[:ND]
    for k in range(K):
        entry = near_ref[k : k + 1, :]
        got = gather(pieces, entry, 0)
        inflow = jnp.where(entry < NP, facing(cosine, sine, coords, got), 0.0)
        inflow_ref[k] = inflow
        for f in range(BAND):
            term = inflow * got[f * STRIDE : f * STRIDE + ND]
            partial_ref[f] = term if k == 0 else partial_ref[f] + term
    along = cosine * wind_ref[0:1, :] + sine * wind_ref[1:2, :]
    for f in range(BAND):
        density = spectra_ref[f]
        up = spectra_ref[f + UP_REACH] if f + UP_REACH < BAND else upper_ref[f + UP_REACH - BAND]
        down = spectra_ref[f - DOWN_REACH] if f >= DOWN_REACH else lower_ref[f]
        up_left, up_right = rolled(up, -UP_SHIFT), rolled(up, UP_SHIFT)
        down_left, down_right = rolled(down, DOWN_SHIFT), rolled(down, -DOWN_SHIFT)
        quad = quad_coupling * (
            density * density * (up_left + down_left + up_right + down_right)
            - 2.0 * density * (up_left * down_left + up_right * down_right)
        )
        growth = wind_growth * jnp.maximum(ratio_of(band, f) * along - 1.0, 0.0)
        base_ref[f] = density + time_step * (quad + growth * density)


def settle(band, f, base, area, total, weight):
    scaled = scale_of(band, f) * area
    return (base + scaled * total) / (1.0 + scaled * weight)


def ghost_pieces(ghost_ref):
    return bf16_pieces(ghost_ref[...].T[:ROWS])


def first_kernel(
    band_ref, ghost_ref, base_ref, partial_ref, inflow_ref, coords_ref, area_ref, near_ref, send_ref, count_ref, table_ref,
    packed_ref, pieces_ref, inflow_out_ref, weight_ref, total_ref, rows_ref,
):
    band = band_ref[0]
    coords = coords_ref[...]
    pieces = ghost_pieces(ghost_ref)
    cosine, sine = wide(table_ref[0])[:ND], wide(table_ref[1])[:ND]
    weight = jnp.zeros((ND, NP), jnp.float32)
    for k in range(K):
        entry = near_ref[k : k + 1, :]
        got = gather(pieces, entry, NP)
        inflow = jnp.where(entry < NP, 0.0, facing(cosine, sine, coords, got))
        both = inflow_ref[k] + inflow
        inflow_out_ref[k] = both
        weight = weight + both
        for f in range(BAND):
            term = inflow * got[f * STRIDE : f * STRIDE + ND]
            total_ref[f] = (partial_ref[f] if k == 0 else total_ref[f]) + term
    weight_ref[...] = weight
    area = area_ref[...]
    fill_rows(rows_ref, [settle(band, f, base_ref[f], area, total_ref[f], weight) for f in range(BAND)], None)
    pieces = bf16_pieces(rows_ref[...])
    pieces_ref[...] = pieces
    packed_ref[:, :ROWS] = pack(pieces, send_ref, count_ref)
    packed_ref[:, ROWS:] = jnp.zeros((GHOSTS, LANES - ROWS), jnp.float32)


def second_local_kernel(pieces_ref, inflow_ref, near_ref, partial_ref):
    pieces = pieces_ref[...]
    for k in range(K):
        got = gather(pieces, near_ref[k : k + 1, :], 0)
        for f in range(BAND):
            term = inflow_ref[k] * got[f * STRIDE : f * STRIDE + ND]
            partial_ref[f] = term if k == 0 else partial_ref[f] + term


def second_kernel(
    band_ref, ghost_ref, base_ref, partial_ref, inflow_ref, weight_ref, area_ref, near_ref, out_ref, total_ref
):
    band = band_ref[0]
    pieces = ghost_pieces(ghost_ref)
    for k in range(K):
        got = gather(pieces, near_ref[k : k + 1, :], NP)
        for f in range(BAND):
            term = inflow_ref[k] * got[f * STRIDE : f * STRIDE + ND]
            total_ref[f] = (partial_ref[f] if k == 0 else total_ref[f]) + term
    area, weight = area_ref[...], weight_ref[...]
    for f in range(BAND):
        out_ref[f] = settle(band, f, base_ref[f], area, total_ref[f], weight)


def call(kernel, outs, scratch, name, scalars, *operands):
    vmem, smem = pl.BlockSpec(memory_space=pltpu.VMEM), pl.BlockSpec(memory_space=pltpu.SMEM)
    return pl.pallas_call(
        kernel,
        out_shape=[jax.ShapeDtypeStruct(shape, dtype) for shape, dtype in outs],
        in_specs=[smem] * len(scalars) + [vmem] * len(operands),
        out_specs=[vmem] * len(outs),
        scratch_shapes=[pltpu.VMEM(shape, jnp.float32) for shape in scratch],
        compiler_params=pltpu.CompilerParams(vmem_limit_bytes=48 << 20),
        name=name,
    )(*scalars, *operands)


def local(spectra, coords, inv_area, wind_vector, neighbours, send_nodes, send_count):
    bands = lax.axis_size("freq")
    band = lax.axis_index("freq").astype(jnp.int32).reshape(1)
    ends = bands - 1
    lower = lax.ppermute(spectra[BAND - DOWN_REACH :], "freq", [(i, i + 1) for i in range(ends)])
    upper = lax.ppermute(spectra[:UP_REACH], "freq", [(i + 1, i) for i in range(ends)])
    angles = (np.arange(STRIDE) + 0.5) * (2.0 * math.pi / ND)
    table = jnp.asarray(
        np.broadcast_to(np.stack([np.cos(angles), np.sin(angles)])[:, :, None], (2, STRIDE, 128)), jnp.float32
    )
    send, count, area = send_nodes.T, send_count.reshape(1, -1), inv_area.reshape(1, -1)
    f32, planes = jnp.float32, (BAND, ND, NP)

    def exchange(packed):
        packed = packed.reshape(N_MESH, CAP, LANES)
        return lax.all_to_all(packed, "mesh", split_axis=0, concat_axis=0, tiled=True).reshape(GHOSTS, LANES)

    (packed,) = call(
        pack_kernel, [((GHOSTS, LANES), f32)], [(ROWS, NP)], "pack", (), spectra, coords, send, count
    )
    ghosts = exchange(packed)
    base, partial, inflow = call(
        local_kernel, [(planes, f32), (planes, f32), ((K, ND, NP), f32)], [(ROWS, NP)], "local_first",
        (band,), spectra, lower, upper, coords, wind_vector, neighbours, table,
    )
    packed, pieces, inflow, weight = call(
        first_kernel,
        [((GHOSTS, LANES), f32), ((2 * ROWS, NP), jnp.bfloat16), ((K, ND, NP), f32), ((ND, NP), f32)],
        [planes, (ROWS, NP)], "first",
        (band,), ghosts, base, partial, inflow, coords, area, neighbours, send, count, table,
    )
    ghosts = exchange(packed)
    (partial,) = call(second_local_kernel, [(planes, f32)], [], "local_second", (), pieces, inflow, neighbours)
    (updated,) = call(
        second_kernel, [(planes, f32)], [planes], "second",
        (band,), ghosts, base, partial, inflow, weight, area, neighbours,
    )
    return updated


def solution(mesh):
    in_specs = (
        P("freq", None, "mesh"),
        P(None, "mesh"),
        P("mesh"),
        P(None, "mesh"),
        P(None, "mesh"),
        P("mesh", None),
        P("mesh"),
    )
    out_specs = P("freq", None, "mesh")
    return jax.shard_map(local, mesh=mesh, in_specs=in_specs, out_specs=out_specs, check_vma=False)
```

profile of v0, /device:TPU:1, one launch (start us, length us, event | category | flops | bytes accessed | tf_op | source)
XLA Modules:
  0.0 62.2 jit_solution(10669496242298035164)
XLA Ops:
  0.0 0.0 copy-start.14
  0.0 0.7 %copy-done.14 = s32[32]{0:T(128)S(1)} copy-done((s32[32]{0:T(128)S(1)}, s32[32]{0:T(128)}, u32[]{:S(2)}) %copy-start.14) | copy-done | bytes 152
  0.7 0.0 copy-start
  0.7 1.1 %copy-done = f32[9,36,512]{2,1,0:T(8,128)S(1)} copy-done((f32[9,36,512]{2,1,0:T(8,128)S(1)}, f32[9,36,512]{2,1,0:T(8,128)}, u32[]{:S(2)}) %copy-start) | copy-done | bytes 663576
  1.8 0.0 copy-start.8
  1.8 0.7 %copy-done.8 = f32[2,512]{1,0:T(2,128)S(1)} copy-done((f32[2,512]{1,0:T(2,128)S(1)}, f32[2,512]{1,0:T(2,128)}, u32[]{:S(2)}) %copy-start.8) | copy-done | bytes 4120
  2.5 0.0 copy-start.10
  2.5 0.7 %copy-done.10 = s32[32,8]{0,1:T(8,128)S(1)} copy-done((s32[32,8]{0,1:T(8,128)S(1)}, s32[32,8]{0,1:T(8,128)}, u32[]{:S(2)}) %copy-start.10) | copy-done | bytes 1048
  3.1 0.0 copy-start.1
  3.1 1.3 %pack.1 = f32[256,384]{1,0:T(8,128)} custom-call(f32[9,36,512]{2,1,0:T(8,128)S(1)} %copy-done, f32[2,512]{1,0:T(2,128)S(1)} %copy-done.8, s32[8,32]{1,0:T(8,128)S(1)} %bitcast.10, s32[1,32]{1,0:T(1,128)S(1)} %bitcast.14), custom_call_target="tpu_custom_call" | custom-call | tf_op jit(solution)/shard_map/pack/pallas_call | solution.py:216
  4.4 11.3 %all-to-all-start = ((f32[32,8,384]{2,1,0:T(8,128)}), f32[32,8,384]{2,1,0:T(8,128)S(1)}, u32[]{:S(2)}, u32[]{:S(2)}) async-start(f32[32,8,384]{2,1,0:T(8,128)} %bitcast.3), calls=%async_computation | async-start | bytes 786432 | tf_op jit(solution)/shard_map/all_to_all | solution.py:242
  15.8 0.0 copy-done.1
  15.8 0.0 copy-start.7
  15.8 3.1 %collective-permute-start = (f32[3,36,512]{2,1,0:T(8,128)S(1)}, f32[3,36,512]{2,1,0:T(8,128)S(1)}, u32[]{:S(2)}, u32[]{:S(2)}) collective-permute-start(f32[3,36,512]{2,1,0:T(8,128)S(1)} %slice.6), channel_id=1, source_target_pairs={{0,1},{1,2},{2,3},{4,5},{5,6},{6,7},{8,9},{9,10},{10,11},{12,13},{... | collective-permute-start | bytes 663560 | tf_op jit(solution)/shard_map/ppermute | solution.py:231
  19.0 0.0 copy-start.6
  19.0 0.0 copy-start.13
  19.0 0.0 copy-start.9
  19.0 1.9 %collective-permute-start.1 = (f32[2,36,512]{2,1,0:T(8,128)S(1)}, f32[2,36,512]{2,1,0:T(8,128)S(1)}, u32[]{:S(2)}, u32[]{:S(2)}) collective-permute-start(f32[2,36,512]{2,1,0:T(8,128)S(1)} %slice.7), channel_id=1, source_target_pairs={{1,0},{2,1},{3,2},{5,4},{6,5},{7,6},{9,8},{10,9},{11,10},{13,12},{... | collective-permute-start | bytes 442376 | tf_op jit(solution)/shard_map/ppermute | solution.py:232
  21.0 5.0 %collective-permute-done.1.upper_ref = f32[2,36,512]{2,1,0:T(8,128)S(1)} collective-permute-done((f32[2,36,512]{2,1,0:T(8,128)S(1)}, f32[2,36,512]{2,1,0:T(8,128)S(1)}, u32[]{:S(2)}, u32[]{:S(2)}) %collective-permute-start.1) | collective-permute-done | bytes 147488 | tf_op jit(solution)/shard_map/ppermute | solution.py:232
  26.0 0.0 collective-permute-done.lower_ref
  26.0 0.0 copy-done.7
  26.0 0.0 copy-done.6
  26.0 0.0 copy-done.13
  26.0 0.0 copy-done.9
  26.0 4.8 %local_first.1 = (f32[9,36,512]{2,1,0:T(8,128)S(1)}, f32[9,36,512]{2,1,0:T(8,128)S(1)}, f32[8,36,512]{2,1,0:T(8,128)S(1)}) custom-call(s32[1]{0:T(128)} %bitcast.band_ref, f32[9,36,512]{2,1,0:T(8,128)S(1)} %copy-done.1, f32[3,36,512]{2,1,0:T(8,128)S(1)} %collective-permute-done.lower_ref, f32[2,36,512]{2,1,0:T(8,128)S(1)} %collective-permute-done.1.upper_ref, ...), custom_call_target="tpu_custom_call" | custom-call | tf_op jit(solution)/shard_map/local_first/pallas_call | solution.py:216
  30.8 0.0 copy-start.2
  30.8 0.9 %copy-done.2 = f32[9,36,512]{2,1,0:T(8,128)} copy-done((f32[9,36,512]{2,1,0:T(8,128)}, f32[9,36,512]{2,1,0:T(8,128)S(1)}, u32[]{:S(2)}) %copy-start.2) | copy-done | bytes 663576
  31.6 0.0 copy-start.4
  31.6 0.9 %copy-done.4 = f32[8,36,512]{2,1,0:T(8,128)} copy-done((f32[8,36,512]{2,1,0:T(8,128)}, f32[8,36,512]{2,1,0:T(8,128)S(1)}, u32[]{:S(2)}) %copy-start.4) | copy-done | bytes 589848
  32.5 0.0 all-to-all-done
  32.5 0.0 copy-start.11
  32.5 0.0 copy-start.12
  32.5 0.7 %copy-done.11 = s32[32,8]{0,1:T(8,128)S(1)} copy-done((s32[32,8]{0,1:T(8,128)S(1)}, s32[32,8]{0,1:T(8,128)}, u32[]{:S(2)}) %copy-start.11) | copy-done | bytes 1048
  33.2 0.0 copy-done.12
  33.2 0.0 copy-start.3
  33.2 1.1 %copy-done.3 = f32[9,36,512]{2,1,0:T(8,128)S(1)} copy-done((f32[9,36,512]{2,1,0:T(8,128)S(1)}, f32[9,36,512]{2,1,0:T(8,128)}, u32[]{:S(2)}) %copy-start.3) | copy-done | bytes 663576
  34.3 0.0 copy-start.5
  34.3 1.1 %copy-done.5 = f32[8,36,512]{2,1,0:T(8,128)S(1)} copy-done((f32[8,36,512]{2,1,0:T(8,128)S(1)}, f32[8,36,512]{2,1,0:T(8,128)}, u32[]{:S(2)}) %copy-start.5) | copy-done | bytes 589848
  35.4 4.1 %first.1 = (f32[256,384]{1,0:T(8,128)}, bf16[736,512]{1,0:T(8,128)(2,1)S(1)}, f32[8,36,512]{2,1,0:T(8,128)S(1)}, f32[36,512]{1,0:T(8,128)S(1)}) custom-call(s32[1]{0:T(128)} %bitcast.band_ref, f32[256,384]{1,0:T(8,128)S(1)} %bitcast.9, f32[9,36,512]{2,1,0:T(8,128)S(1)} %get-tuple-element.12.base_ref, f32[9,36,512]{2,1,0:T(8,128)S(1)} %copy-done.3, ...), custom_call_target="tpu_custom_call" | custom-call | tf_op jit(solution)/shard_map/first/pallas_call | solution.py:216
  39.5 10.0 %all-to-all-start.1 = ((f32[32,8,384]{2,1,0:T(8,128)}), f32[32,8,384]{2,1,0:T(8,128)S(1)}, u32[]{:S(2)}, u32[]{:S(2)}) async-start(f32[32,8,384]{2,1,0:T(8,128)} %bitcast.6), calls=%async_computation.1 | async-start | bytes 786432 | tf_op jit(solution)/shard_map/all_to_all | solution.py:242
  49.5 3.3 %local_second.1.partial_ref = f32[9,36,512]{2,1,0:T(8,128)S(1)} custom-call(bf16[736,512]{1,0:T(8,128)(2,1)S(1)} %get-tuple-element.16.pieces_ref, f32[8,36,512]{2,1,0:T(8,128)S(1)} %get-tuple-element.17.inflow_ref, s32[8,512]{1,0:T(8,128)S(1)} %copy-done.6), custom_call_target="tpu_custom_call" | custom-call | tf_op jit(solution)/shard_map/local_second/pallas_call | solution.py:216
  52.8 6.6 %all-to-all-done.1 = f32[32,8,384]{2,1,0:T(8,128)S(1)} async-done(((f32[32,8,384]{2,1,0:T(8,128)}), f32[32,8,384]{2,1,0:T(8,128)S(1)}, u32[]{:S(2)}, u32[]{:S(2)}) %all-to-all-start.1) | async-done | bytes 393248 | tf_op jit(solution)/shard_map/all_to_all | solution.py:242
  59.4 2.8 %second.1 = f32[9,36,512]{2,1,0:T(8,128)} custom-call(s32[1]{0:T(128)} %bitcast.band_ref, f32[256,384]{1,0:T(8,128)S(1)} %bitcast.8, f32[9,36,512]{2,1,0:T(8,128)S(1)} %get-tuple-element.12.base_ref, f32[9,36,512]{2,1,0:T(8,128)S(1)} %local_second.1.partial_ref, f32[8,36,512]{2,1,0:T(8,128)S(1)} %get-tuple-element.17.inflow_ref, ...), custom_call_target="tpu_custom_call" | custom-call | tf_op jit(solution)/shard_map/second/pallas_call | solution.py:216
  (2 shorter events, 0.0 us)
Async XLA Ops:
  0.0 0.7 %copy-start.14 = (s32[32]{0:T(128)S(1)}, s32[32]{0:T(128)}, u32[]{:S(2)}) copy-start(s32[32]{0:T(128)} %param.14) | copy-start | bytes 388
  0.7 1.1 %copy-start = (f32[9,36,512]{2,1,0:T(8,128)S(1)}, f32[9,36,512]{2,1,0:T(8,128)}, u32[]{:S(2)}) copy-start(f32[9,36,512]{2,1,0:T(8,128)} %spectra_ref.3) | copy-start | bytes 1990660
  1.8 0.7 %copy-start.8 = (f32[2,512]{1,0:T(2,128)S(1)}, f32[2,512]{1,0:T(2,128)}, u32[]{:S(2)}) copy-start(f32[2,512]{1,0:T(2,128)} %coords_ref.5) | copy-start | bytes 12292
  2.5 0.7 %copy-start.10 = (s32[32,8]{0,1:T(8,128)S(1)}, s32[32,8]{0,1:T(8,128)}, u32[]{:S(2)}) copy-start(s32[32,8]{0,1:T(8,128)} %param.13) | copy-start | bytes 3076
  3.1 12.6 %copy-start.1 = (f32[9,36,512]{2,1,0:T(8,128)S(1)}, f32[9,36,512]{2,1,0:T(8,128)}, u32[]{:S(2)}) copy-start(f32[9,36,512]{2,1,0:T(8,128)} %spectra_ref.3) | copy-start | bytes 1990660
  4.4 28.1 %all-to-all-start = ((f32[32,8,384]{2,1,0:T(8,128)}), f32[32,8,384]{2,1,0:T(8,128)S(1)}, u32[]{:S(2)}, u32[]{:S(2)}) async-start(f32[32,8,384]{2,1,0:T(8,128)} %bitcast.3), calls=%async_computation | async-start | bytes 786432 | tf_op jit(solution)/shard_map/all_to_all | solution.py:242
  15.8 10.2 %copy-start.7 = (f32[2,40,128]{2,1,0:T(8,128)S(1)}, f32[2,40,128]{2,1,0:T(8,128)}, u32[]{:S(2)}) copy-start(f32[2,40,128]{2,1,0:T(8,128)} %constant.6.clone.table_ref) | copy-start | bytes 122884
  15.8 10.1 %collective-permute-start = (f32[3,36,512]{2,1,0:T(8,128)S(1)}, f32[3,36,512]{2,1,0:T(8,128)S(1)}, u32[]{:S(2)}, u32[]{:S(2)}) collective-permute-start(f32[3,36,512]{2,1,0:T(8,128)S(1)} %slice.6), channel_id=1, source_target_pairs={{0,1},{1,2},{2,3},{4,5},{5,6},{6,7},{8,9},{9,10},{10,11},{12,13},{... | collective-permute-start | bytes 663560 | tf_op jit(solution)/shard_map/ppermute | solution.py:231
  19.0 7.0 %copy-start.6 = (s32[8,512]{1,0:T(8,128)S(1)}, s32[8,512]{1,0:T(8,128)}, u32[]{:S(2)}) copy-start(s32[8,512]{1,0:T(8,128)} %near_ref.7) | copy-start | bytes 49156
  19.0 7.0 %copy-start.13 = (f32[2,512]{1,0:T(2,128)S(1)}, f32[2,512]{1,0:T(2,128)}, u32[]{:S(2)}) copy-start(f32[2,512]{1,0:T(2,128)} %wind_ref.1) | copy-start | bytes 12292
  19.0 7.0 %copy-start.9 = (f32[2,512]{1,0:T(2,128)S(1)}, f32[2,512]{1,0:T(2,128)}, u32[]{:S(2)}) copy-start(f32[2,512]{1,0:T(2,128)} %coords_ref.5) | copy-start | bytes 12292
  19.0 6.9 %collective-permute-start.1 = (f32[2,36,512]{2,1,0:T(8,128)S(1)}, f32[2,36,512]{2,1,0:T(8,128)S(1)}, u32[]{:S(2)}, u32[]{:S(2)}) collective-permute-start(f32[2,36,512]{2,1,0:T(8,128)S(1)} %slice.7), channel_id=1, source_target_pairs={{1,0},{2,1},{3,2},{5,4},{6,5},{7,6},{9,8},{10,9},{11,10},{13,12},{... | collective-permute-start | bytes 442376 | tf_op jit(solution)/shard_map/ppermute | solution.py:232
  30.8 0.9 %copy-start.2 = (f32[9,36,512]{2,1,0:T(8,128)}, f32[9,36,512]{2,1,0:T(8,128)S(1)}, u32[]{:S(2)}) copy-start(f32[9,36,512]{2,1,0:T(8,128)S(1)} %get-tuple-element.13.partial_ref) | copy-start | bytes 1990660
  31.6 0.9 %copy-start.4 = (f32[8,36,512]{2,1,0:T(8,128)}, f32[8,36,512]{2,1,0:T(8,128)S(1)}, u32[]{:S(2)}) copy-start(f32[8,36,512]{2,1,0:T(8,128)S(1)} %get-tuple-element.14.inflow_ref) | copy-start | bytes 1769476
  32.5 0.7 %copy-start.11 = (s32[32,8]{0,1:T(8,128)S(1)}, s32[32,8]{0,1:T(8,128)}, u32[]{:S(2)}) copy-start(s32[32,8]{0,1:T(8,128)} %param.13) | copy-start | bytes 3076
  32.5 0.7 %copy-start.12 = (f32[512]{0:T(512)S(1)}, f32[512]{0:T(512)}, u32[]{:S(2)}) copy-start(f32[512]{0:T(512)} %param.10) | copy-start | bytes 6148
  33.2 1.1 %copy-start.3 = (f32[9,36,512]{2,1,0:T(8,128)S(1)}, f32[9,36,512]{2,1,0:T(8,128)}, u32[]{:S(2)}) copy-start(f32[9,36,512]{2,1,0:T(8,128)} %copy-done.2) | copy-start | bytes 1990660
  34.3 1.1 %copy-start.5 = (f32[8,36,512]{2,1,0:T(8,128)S(1)}, f32[8,36,512]{2,1,0:T(8,128)}, u32[]{:S(2)}) copy-start(f32[8,36,512]{2,1,0:T(8,128)} %copy-done.4) | copy-start | bytes 1769476
  39.5 19.9 %all-to-all-start.1 = ((f32[32,8,384]{2,1,0:T(8,128)}), f32[32,8,384]{2,1,0:T(8,128)S(1)}, u32[]{:S(2)}, u32[]{:S(2)}) async-start(f32[32,8,384]{2,1,0:T(8,128)} %bitcast.6), calls=%async_computation.1 | async-start | bytes 786432 | tf_op jit(solution)/shard_map/all_to_all | solution.py:242
where the time goes:
time: 62.8 us; the launch traced here: 62.2 us
  starting transfers between devices  26.4 us (42%)
  Pallas kernels  16.2 us (26%)
  waiting for transfers between devices  11.6 us (18%)
  local copies, waits for them, and re-layouts  7.83 us (12%)
    all_to_all x2, starting transfers between devices, exchange(): lax.all_to_all(packed, 'mesh', split_axis=0, concat_axis=0, tiled=True)  21.4 us
    pallas_call x5, Pallas kernels, call(): pl.pallas_call(kernel, out_shape=[jax.ShapeDtypeStruct(shape, dtype) for...  16.2 us
    unnamed x30, local copies, waits for them, and re-layouts  7.8 us
    all_to_all x2, waiting for transfers between devices, exchange(): lax.all_to_all(packed, 'mesh', split_axis=0, concat_axis=0, tiled=True)  6.6 us
    ppermute x1, waiting for transfers between devices, local(): lax.ppermute(spectra[:UP_REACH], 'freq', [(i + 1, i) for i in range(ends)])  5 us
    ppermute x1, starting transfers between devices, local(): lax.ppermute(spectra[BAND - DOWN_REACH:], 'freq', [(i, i + 1) for i in ra...  3.15 us
    ppermute x1, starting transfers between devices, local(): lax.ppermute(spectra[:UP_REACH], 'freq', [(i + 1, i) for i in range(ends)])  1.92 us
  transfers between devices with their start and end apart: 4, of which 2 were waited for; matrix products, arithmetic and copies ran while one was open for 0% of the time, Pallas kernels for 13%

commit v1 on v0

--- a/solution.py
+++ b/solution.py
@@ -100,16 +100,25 @@
     return jnp.concatenate([table] * (NP // 128), axis=1)
 
 
-def pack_kernel(spectra_ref, coords_ref, send_ref, count_ref, out_ref, rows_ref):
+def pack_kernel(*refs):
+    sources, out_ref, rows_ref, buffers, sems = refs[:4], refs[4], refs[5], refs[6:10], refs[10]
+    copies = [pltpu.make_async_copy(sources[i], buffers[i], sems.at[i]) for i in range(4)]
+    for copy in copies:
+        copy.start()
+    for copy in copies:
+        copy.wait()
+    spectra_ref, coords_ref, send_ref, count_ref = buffers
     fill_rows(rows_ref, [spectra_ref[f] for f in range(BAND)], coords_ref[...])
     out_ref[:, :ROWS] = pack(bf16_pieces(rows_ref[...]), send_ref, count_ref)
     out_ref[:, ROWS:] = jnp.zeros((GHOSTS, LANES - ROWS), jnp.float32)
 
 
-def facing(cosine, sine, coords, got):
-    base = BAND * STRIDE
-    delta_x = (got[base : base + 1] + got[base + 1 : base + 2]) - coords[0:1]
-    delta_y = (got[base + 2 : base + 3] + got[base + 3 : base + 4]) - coords[1:2]
+def delta(got, coords, axis):
+    base = BAND * STRIDE + 2 * axis
+    return (got[base : base + 1] + got[base + 1 : base + 2]) - coords[axis : axis + 1]
+
+
+def facing(cosine, sine, delta_x, delta_y):
     return jnp.maximum(-(cosine * delta_x + sine * delta_y), 0.0)
 
 
@@ -119,8 +128,8 @@
 
 
 def local_kernel(
-    band_ref, spectra_ref, lower_ref, upper_ref, coords_ref, wind_ref, near_ref, table_ref,
-    base_ref, partial_ref, inflow_ref, rows_ref,
+    band_ref, spectra_ref, lower_ref, upper_ref, coords_ref, wind_ref, area_ref, near_ref, table_ref,
+    base_ref, partial_ref, rows_ref,
 ):
     band = band_ref[0]
     coords = coords_ref[...]
@@ -130,11 +139,15 @@
     for k in range(K):
         entry = near_ref[k : k + 1, :]
         got = gather(pieces, entry, 0)
-        inflow = jnp.where(entry < NP, facing(cosine, sine, coords, got), 0.0)
-        inflow_ref[k] = inflow
+        delta_x = jnp.where(entry < NP, delta(got, coords, 0), 0.0)
+        delta_y = jnp.where(entry < NP, delta(got, coords, 1), 0.0)
+        partial_ref[k, ND : ND + 1] = delta_x
+        partial_ref[k, ND + 1 : ND + 2] = delta_y
+        inflow = facing(cosine, sine, delta_x, delta_y)
         for f in range(BAND):
             term = inflow * got[f * STRIDE : f * STRIDE + ND]
-            partial_ref[f] = term if k == 0 else partial_ref[f] + term
+            partial_ref[f, :ND] = term if k == 0 else partial_ref[f, :ND] + term
+    partial_ref[K, ND : ND + 1] = area_ref[...]
     along = cosine * wind_ref[0:1, :] + sine * wind_ref[1:2, :]
     for f in range(BAND):
         density = spectra_ref[f]
@@ -160,8 +173,8 @@
 
 
 def first_kernel(
-    band_ref, ghost_ref, base_ref, partial_ref, inflow_ref, coords_ref, area_ref, near_ref, send_ref, count_ref, table_ref,
-    packed_ref, pieces_ref, inflow_out_ref, weight_ref, total_ref, rows_ref,
+    band_ref, ghost_ref, base_ref, partial_ref, coords_ref, near_ref, send_ref, count_ref, table_ref,
+    packed_ref, pieces_ref, delta_ref, total_ref, rows_ref,
 ):
     band = band_ref[0]
     coords = coords_ref[...]
@@ -171,15 +184,17 @@
     for k in range(K):
         entry = near_ref[k : k + 1, :]
         got = gather(pieces, entry, NP)
-        inflow = jnp.where(entry < NP, 0.0, facing(cosine, sine, coords, got))
-        both = inflow_ref[k] + inflow
-        inflow_out_ref[k] = both
-        weight = weight + both
+        delta_x = jnp.where(entry < NP, partial_ref[k, ND : ND + 1], delta(got, coords, 0))
+        delta_y = jnp.where(entry < NP, partial_ref[k, ND + 1 : ND + 2], delta(got, coords, 1))
+        delta_ref[k : k + 1, :] = delta_x
+        delta_ref[K + k : K + k + 1, :] = delta_y
+        inflow = facing(cosine, sine, delta_x, delta_y)
+        weight = weight + inflow
         for f in range(BAND):
             term = inflow * got[f * STRIDE : f * STRIDE + ND]
-            total_ref[f] = (partial_ref[f] if k == 0 else total_ref[f]) + term
-    weight_ref[...] = weight
-    area = area_ref[...]
+            total_ref[f] = (partial_ref[f, :ND] if k == 0 else total_ref[f]) + term
+    area = partial_ref[K, ND : ND + 1]
+    delta_ref[2 * K : 2 * K + 1, :] = area
     fill_rows(rows_ref, [settle(band, f, base_ref[f], area, total_ref[f], weight) for f in range(BAND)], None)
     pieces = bf16_pieces(rows_ref[...])
     pieces_ref[...] = pieces
@@ -187,26 +202,32 @@
     packed_ref[:, ROWS:] = jnp.zeros((GHOSTS, LANES - ROWS), jnp.float32)
 
 
-def second_local_kernel(pieces_ref, inflow_ref, near_ref, partial_ref):
+def second_local_kernel(pieces_ref, delta_ref, near_ref, table_ref, partial_ref):
     pieces = pieces_ref[...]
+    cosine, sine = wide(table_ref[0])[:ND], wide(table_ref[1])[:ND]
     for k in range(K):
         got = gather(pieces, near_ref[k : k + 1, :], 0)
+        inflow = facing(cosine, sine, delta_ref[k : k + 1, :], delta_ref[K + k : K + k + 1, :])
         for f in range(BAND):
-            term = inflow_ref[k] * got[f * STRIDE : f * STRIDE + ND]
+            term = inflow * got[f * STRIDE : f * STRIDE + ND]
             partial_ref[f] = term if k == 0 else partial_ref[f] + term
 
 
 def second_kernel(
-    band_ref, ghost_ref, base_ref, partial_ref, inflow_ref, weight_ref, area_ref, near_ref, out_ref, total_ref
+    band_ref, ghost_ref, base_ref, partial_ref, delta_ref, near_ref, table_ref, out_ref, total_ref
 ):
     band = band_ref[0]
     pieces = ghost_pieces(ghost_ref)
+    cosine, sine = wide(table_ref[0])[:ND], wide(table_ref[1])[:ND]
+    weight = jnp.zeros((ND, NP), jnp.float32)
     for k in range(K):
         got = gather(pieces, near_ref[k : k + 1, :], NP)
+        inflow = facing(cosine, sine, delta_ref[k : k + 1, :], delta_ref[K + k : K + k + 1, :])
+        weight = weight + inflow
         for f in range(BAND):
-            term = inflow_ref[k] * got[f * STRIDE : f * STRIDE + ND]
+            term = inflow * got[f * STRIDE : f * STRIDE + ND]
             total_ref[f] = (partial_ref[f] if k == 0 else total_ref[f]) + term
-    area, weight = area_ref[...], weight_ref[...]
+    area = delta_ref[2 * K : 2 * K + 1, :]
     for f in range(BAND):
         out_ref[f] = settle(band, f, base_ref[f], area, total_ref[f], weight)
 
@@ -219,7 +240,7 @@
         in_specs=[smem] * len(scalars) + [vmem] * len(operands),
         out_specs=[vmem] * len(outs),
         scratch_shapes=[pltpu.VMEM(shape, jnp.float32) for shape in scratch],
-        compiler_params=pltpu.CompilerParams(vmem_limit_bytes=48 << 20),
+        compiler_params=pltpu.CompilerParams(vmem_limit_bytes=24 << 20),
         name=name,
     )(*scalars, *operands)
 
@@ -241,25 +262,37 @@
         packed = packed.reshape(N_MESH, CAP, LANES)
         return lax.all_to_all(packed, "mesh", split_axis=0, concat_axis=0, tiled=True).reshape(GHOSTS, LANES)
 
-    (packed,) = call(
-        pack_kernel, [((GHOSTS, LANES), f32)], [(ROWS, NP)], "pack", (), spectra, coords, send, count
-    )
+    inputs = (spectra, coords, send, count)
+    packed = pl.pallas_call(
+        pack_kernel,
+        out_shape=jax.ShapeDtypeStruct((GHOSTS, LANES), f32),
+        in_specs=[pl.BlockSpec(memory_space=pltpu.HBM)] * len(inputs),
+        out_specs=pl.BlockSpec(memory_space=pltpu.VMEM),
+        scratch_shapes=[
+            pltpu.VMEM((ROWS, NP), f32),
+            *[pltpu.VMEM(x.shape, x.dtype) for x in inputs],
+            pltpu.SemaphoreType.DMA((len(inputs),)),
+        ],
+        compiler_params=pltpu.CompilerParams(vmem_limit_bytes=24 << 20),
+        name="pack",
+    )(*inputs)
+    packed, lower, upper = lax.optimization_barrier((packed, lower, upper))
     ghosts = exchange(packed)
-    base, partial, inflow = call(
-        local_kernel, [(planes, f32), (planes, f32), ((K, ND, NP), f32)], [(ROWS, NP)], "local_first",
-        (band,), spectra, lower, upper, coords, wind_vector, neighbours, table,
-    )
-    packed, pieces, inflow, weight = call(
+    base, partial = call(
+        local_kernel, [(planes, f32), ((BAND, STRIDE, NP), f32)], [(ROWS, NP)], "local_first",
+        (band,), spectra, lower, upper, coords, wind_vector, area, neighbours, table,
+    )
+    packed, pieces, deltas = call(
         first_kernel,
-        [((GHOSTS, LANES), f32), ((2 * ROWS, NP), jnp.bfloat16), ((K, ND, NP), f32), ((ND, NP), f32)],
+        [((GHOSTS, LANES), f32), ((2 * ROWS, NP), jnp.bfloat16), ((3 * K, NP), f32)],
         [planes, (ROWS, NP)], "first",
-        (band,), ghosts, base, partial, inflow, coords, area, neighbours, send, count, table,
+        (band,), ghosts, base, partial, coords, neighbours, send, count, table,
     )
     ghosts = exchange(packed)
-    (partial,) = call(second_local_kernel, [(planes, f32)], [], "local_second", (), pieces, inflow, neighbours)
+    (partial,) = call(second_local_kernel, [(planes, f32)], [], "local_second", (), pieces, deltas, neighbours, table)
     (updated,) = call(
         second_kernel, [(planes, f32)], [planes], "second",
-        (band,), ghosts, base, partial, inflow, weight, area, neighbours,
+        (band,), ghosts, base, partial, deltas, neighbours, table,
     )
     return updated
 

time: 62.8 us -> 55.2 us (0.88)
  starting transfers between devices: 26.4 us -> 21.4 us
  local copies, waits for them, and re-layouts: 7.83 us -> 3.28 us
  waiting for transfers between devices: 11.6 us -> 14.2 us
    unnamed x30 -> x16, local copies, waits for them, and re-layouts: 7.8 us -> 1.31 us
    all_to_all x2, starting transfers between devices: 21.4 us -> 14.9 us  [exchange(): lax.all_to_all(packed, 'mesh', split_axis=0, concat_axis=0, tiled=True)]
    all_to_all x2, waiting for transfers between devices: 6.6 us -> 11.8 us  [exchange(): lax.all_to_all(packed, 'mesh', split_axis=0, concat_axis=0, tiled=True)]
    ppermute x1, waiting for transfers between devices: 5 us -> 2.42 us  [local(): lax.ppermute(spectra[:UP_REACH], 'freq', [(i + 1, i) for i in range(ends)])]
    pallas_call x5 -> x4, Pallas kernels: 16.2 us -> 14.1 us  [call(): pl.pallas_call(kernel, out_shape=[jax.ShapeDtypeStruct(shape, dtype) for...]
    pallas_call x0 -> x1, Pallas kernels: none -> 1.62 us  [local(): pl.pallas_call(pack_kernel, out_shape=jax.ShapeDtypeStruct((GHOSTS, LANES...]
    ppermute x1, starting transfers between devices: 3.15 us -> 4.59 us  [local(): lax.ppermute(spectra[BAND - DOWN_REACH:], 'freq', [(i, i + 1) for i in ra...]
    slice x1, local copies, waits for them, and re-layouts: 0.02 us -> 1.03 us  [local(): spectra[BAND - DOWN_REACH:]]
  transfers between devices with their start and end apart: 4 -> 4, of which waited for: 2 -> 3; matrix products, arithmetic and copies ran while one was open for 0% -> 2% of each run, Pallas kernels for 13% -> 17%
where the time goes in v1:
time: 55.2 us; the launch traced here: 54.7 us
  starting transfers between devices  21.4 us (39%)
  Pallas kernels  15.7 us (28%)
  waiting for transfers between devices  14.2 us (26%)
  local copies, waits for them, and re-layouts  3.28 us (6%)
    all_to_all x2, starting transfers between devices, exchange(): lax.all_to_all(packed, 'mesh', split_axis=0, concat_axis=0, tiled=True)  14.9 us
    pallas_call x4, Pallas kernels, call(): pl.pallas_call(kernel, out_shape=[jax.ShapeDtypeStruct(shape, dtype) for...  14.1 us
    all_to_all x2, waiting for transfers between devices, exchange(): lax.all_to_all(packed, 'mesh', split_axis=0, concat_axis=0, tiled=True)  11.8 us
    ppermute x1, starting transfers between devices, local(): lax.ppermute(spectra[BAND - DOWN_REACH:], 'freq', [(i, i + 1) for i in ra...  4.59 us
    ppermute x1, waiting for transfers between devices, local(): lax.ppermute(spectra[:UP_REACH], 'freq', [(i + 1, i) for i in range(ends)])  2.42 us
    ppermute x1, starting transfers between devices, local(): lax.ppermute(spectra[:UP_REACH], 'freq', [(i + 1, i) for i in range(ends)])  1.92 us
    pallas_call x1, Pallas kernels, local(): pl.pallas_call(pack_kernel, out_shape=jax.ShapeDtypeStruct((GHOSTS, LANES...  1.62 us
    unnamed x16, local copies, waits for them, and re-layouts  1.31 us
  transfers between devices with their start and end apart: 4, of which 3 were waited for; matrix products, arithmetic and copies ran while one was open for 2% of the time, Pallas kernels for 17%

profile of v1, /device:TPU:1, one launch (start us, length us, event | category | flops | bytes accessed | tf_op | source)
XLA Modules:
  0.0 54.7 jit_solution(2367252852362666342)
XLA Ops:
  0.0 0.0 copy-start
  0.0 1.0 %slice.6 = f32[3,36,512]{2,1,0:T(8,128)S(1)} slice(f32[9,36,512]{2,1,0:T(8,128)} %spectra_ref.1), slice={[6:9], [0:36], [0:512]} | slice | bytes 442368 | tf_op jit(solution)/shard_map/slice | solution.py:252
  1.0 4.6 %collective-permute-start = (f32[3,36,512]{2,1,0:T(8,128)S(1)}, f32[3,36,512]{2,1,0:T(8,128)S(1)}, u32[]{:S(2)}, u32[]{:S(2)}) collective-permute-start(f32[3,36,512]{2,1,0:T(8,128)S(1)} %slice.6), channel_id=1, source_target_pairs={{0,1},{1,2},{2,3},{4,5},{5,6},{6,7},{8,9},{9,10},{10,11},{12,13},{... | collective-permute-start | bytes 663560 | tf_op jit(solution)/shard_map/ppermute | solution.py:252
  5.6 0.0 copy-start.3
  5.7 0.0 copy-start.4
  5.7 0.9 %slice.7 = f32[2,36,512]{2,1,0:T(8,128)S(1)} slice(f32[9,36,512]{2,1,0:T(8,128)} %spectra_ref.1), slice={[0:2], [0:36], [0:512]} | slice | bytes 294912 | tf_op jit(solution)/shard_map/slice | solution.py:253
  6.6 1.9 %collective-permute-start.1 = (f32[2,36,512]{2,1,0:T(8,128)S(1)}, f32[2,36,512]{2,1,0:T(8,128)S(1)}, u32[]{:S(2)}, u32[]{:S(2)}) collective-permute-start(f32[2,36,512]{2,1,0:T(8,128)S(1)} %slice.7), channel_id=1, source_target_pairs={{1,0},{2,1},{3,2},{5,4},{6,5},{7,6},{9,8},{10,9},{11,10},{13,12},{... | collective-permute-start | bytes 442376 | tf_op jit(solution)/shard_map/ppermute | solution.py:253
  8.5 0.0 copy-start.7
  8.5 0.0 copy-done
  8.6 0.0 copy-done.3
  8.6 0.0 copy-done.4
  8.6 0.6 %copy-done.7 = s32[32]{0:T(128)S(1)} copy-done((s32[32]{0:T(128)S(1)}, s32[32]{0:T(128)}, u32[]{:S(2)}) %copy-start.7) | copy-done | bytes 152
  9.2 1.6 %pack.1 = f32[256,384]{1,0:T(8,128)} custom-call(f32[9,36,512]{2,1,0:T(8,128)S(1)} %copy-done, f32[2,512]{1,0:T(2,128)S(1)} %copy-done.3, s32[8,32]{1,0:T(8,128)S(1)} %bitcast.10, s32[1,32]{1,0:T(1,128)S(1)} %bitcast.13), custom_call_target="tpu_custom_call" | custom-call | tf_op jit(solution)/shard_map/pack/pallas_call | solution.py:266
  10.8 2.4 %collective-permute-done.1.upper_ref = f32[2,36,512]{2,1,0:T(8,128)S(1)} collective-permute-done((f32[2,36,512]{2,1,0:T(8,128)S(1)}, f32[2,36,512]{2,1,0:T(8,128)S(1)}, u32[]{:S(2)}, u32[]{:S(2)}) %collective-permute-start.1) | collective-permute-done | bytes 147488 | tf_op jit(solution)/shard_map/ppermute | solution.py:253
  13.2 0.0 collective-permute-done.lower_ref
  13.2 0.0 copy-start.1
  13.2 0.0 copy-start.2
  13.3 10.4 %all-to-all-start = ((f32[32,8,384]{2,1,0:T(8,128)}), f32[32,8,384]{2,1,0:T(8,128)S(1)}, u32[]{:S(2)}, u32[]{:S(2)}) async-start(f32[32,8,384]{2,1,0:T(8,128)} %bitcast.3), calls=%async_computation | async-start | bytes 786432 | tf_op jit(solution)/shard_map/all_to_all | solution.py:263
  23.6 0.0 copy-start.5
  23.6 0.0 copy-start.6
  23.6 0.0 copy-done.1
  23.7 0.0 copy-done.2
  23.7 0.6 %copy-done.5 = f32[2,512]{1,0:T(2,128)S(1)} copy-done((f32[2,512]{1,0:T(2,128)S(1)}, f32[2,512]{1,0:T(2,128)}, u32[]{:S(2)}) %copy-start.5) | copy-done | bytes 4120
  24.3 0.0 copy-done.6
  24.3 4.5 %local_first.1 = (f32[9,36,512]{2,1,0:T(8,128)S(1)}, f32[9,40,512]{2,1,0:T(8,128)S(1)}) custom-call(s32[1]{0:T(128)} %bitcast.band_ref, f32[9,36,512]{2,1,0:T(8,128)S(1)} %copy-done, f32[3,36,512]{2,1,0:T(8,128)S(1)} %collective-permute-done.lower_ref, f32[2,36,512]{2,1,0:T(8,128)S(1)} %collective-permute-done.1.upper_ref, f32[2,512]{1,0:T(2,128)S(1)} %copy-done.3, ...), custom_call_target="tpu_custom_call" | custom-call | tf_op jit(solution)/shard_map/local_first/pallas_call | solution.py:237
  28.8 4.9 %all-to-all-done = f32[32,8,384]{2,1,0:T(8,128)S(1)} async-done(((f32[32,8,384]{2,1,0:T(8,128)}), f32[32,8,384]{2,1,0:T(8,128)S(1)}, u32[]{:S(2)}, u32[]{:S(2)}) %all-to-all-start) | async-done | bytes 393248 | tf_op jit(solution)/shard_map/all_to_all | solution.py:263
  33.7 3.5 %first.1 = (f32[256,384]{1,0:T(8,128)}, bf16[736,512]{1,0:T(8,128)(2,1)S(1)}, f32[24,512]{1,0:T(8,128)S(1)}) custom-call(s32[1]{0:T(128)} %bitcast.band_ref, f32[256,384]{1,0:T(8,128)S(1)} %bitcast.8, f32[9,36,512]{2,1,0:T(8,128)S(1)} %get-tuple-element.16.base_ref, f32[9,40,512]{2,1,0:T(8,128)S(1)} %get-tuple-element.17.partial_ref, ...), custom_call_target="tpu_custom_call" | custom-call | tf_op jit(solution)/shard_map/first/pallas_call | solution.py:237
  37.2 4.5 %all-to-all-start.1 = ((f32[32,8,384]{2,1,0:T(8,128)}), f32[32,8,384]{2,1,0:T(8,128)S(1)}, u32[]{:S(2)}, u32[]{:S(2)}) async-start(f32[32,8,384]{2,1,0:T(8,128)} %bitcast.6), calls=%async_computation.1 | async-start | bytes 786432 | tf_op jit(solution)/shard_map/all_to_all | solution.py:263
  41.8 3.3 %local_second.1.partial_ref = f32[9,36,512]{2,1,0:T(8,128)S(1)} custom-call(bf16[736,512]{1,0:T(8,128)(2,1)S(1)} %get-tuple-element.19.pieces_ref, f32[24,512]{1,0:T(8,128)S(1)} %get-tuple-element.20.delta_ref, s32[8,512]{1,0:T(8,128)S(1)} %copy-done.2, f32[2,40,128]{2,1,0:T(8,128)S(1)} %copy-done.1), custom_call_target="tpu_custom_call" | custom-call | tf_op jit(solution)/shard_map/local_second/pallas_call | solution.py:237
  45.1 6.9 %all-to-all-done.1 = f32[32,8,384]{2,1,0:T(8,128)S(1)} async-done(((f32[32,8,384]{2,1,0:T(8,128)}), f32[32,8,384]{2,1,0:T(8,128)S(1)}, u32[]{:S(2)}, u32[]{:S(2)}) %all-to-all-start.1) | async-done | bytes 393248 | tf_op jit(solution)/shard_map/all_to_all | solution.py:263
  52.0 2.8 %second.1 = f32[9,36,512]{2,1,0:T(8,128)} custom-call(s32[1]{0:T(128)} %bitcast.band_ref, f32[256,384]{1,0:T(8,128)S(1)} %bitcast.9, f32[9,36,512]{2,1,0:T(8,128)S(1)} %get-tuple-element.16.base_ref, f32[9,36,512]{2,1,0:T(8,128)S(1)} %local_second.1.partial_ref, f32[24,512]{1,0:T(8,128)S(1)} %get-tuple-element.20.delta_ref, s32[8,512]{1,0:T(8,128)S(1)} %copy-done.2, ...), custom_call_target="tpu_custom_call" | custom-call | tf_op jit(solution)/shard_map/second/pallas_call | solution.py:237
Async XLA Ops:
  0.0 8.5 %copy-start = (f32[9,36,512]{2,1,0:T(8,128)S(1)}, f32[9,36,512]{2,1,0:T(8,128)}, u32[]{:S(2)}) copy-start(f32[9,36,512]{2,1,0:T(8,128)} %spectra_ref.1) | copy-start | bytes 1990660
  1.0 12.2 %collective-permute-start = (f32[3,36,512]{2,1,0:T(8,128)S(1)}, f32[3,36,512]{2,1,0:T(8,128)S(1)}, u32[]{:S(2)}, u32[]{:S(2)}) collective-permute-start(f32[3,36,512]{2,1,0:T(8,128)S(1)} %slice.6), channel_id=1, source_target_pairs={{0,1},{1,2},{2,3},{4,5},{5,6},{6,7},{8,9},{9,10},{10,11},{12,13},{... | collective-permute-start | bytes 663560 | tf_op jit(solution)/shard_map/ppermute | solution.py:252
  5.6 2.9 %copy-start.3 = (f32[2,512]{1,0:T(2,128)S(1)}, f32[2,512]{1,0:T(2,128)}, u32[]{:S(2)}) copy-start(f32[2,512]{1,0:T(2,128)} %coords_ref.3) | copy-start | bytes 12292
  5.7 2.9 %copy-start.4 = (s32[32,8]{0,1:T(8,128)S(1)}, s32[32,8]{0,1:T(8,128)}, u32[]{:S(2)}) copy-start(s32[32,8]{0,1:T(8,128)} %param.13) | copy-start | bytes 3076
  6.6 6.6 %collective-permute-start.1 = (f32[2,36,512]{2,1,0:T(8,128)S(1)}, f32[2,36,512]{2,1,0:T(8,128)S(1)}, u32[]{:S(2)}, u32[]{:S(2)}) collective-permute-start(f32[2,36,512]{2,1,0:T(8,128)S(1)} %slice.7), channel_id=1, source_target_pairs={{1,0},{2,1},{3,2},{5,4},{6,5},{7,6},{9,8},{10,9},{11,10},{13,12},{... | collective-permute-start | bytes 442376 | tf_op jit(solution)/shard_map/ppermute | solution.py:253
  8.5 0.7 %copy-start.7 = (s32[32]{0:T(128)S(1)}, s32[32]{0:T(128)}, u32[]{:S(2)}) copy-start(s32[32]{0:T(128)} %param.14) | copy-start | bytes 388
  13.2 10.4 %copy-start.1 = (f32[2,40,128]{2,1,0:T(8,128)S(1)}, f32[2,40,128]{2,1,0:T(8,128)}, u32[]{:S(2)}) copy-start(f32[2,40,128]{2,1,0:T(8,128)} %constant.6.clone.table_ref) | copy-start | bytes 122884
  13.2 10.4 %copy-start.2 = (s32[8,512]{1,0:T(8,128)S(1)}, s32[8,512]{1,0:T(8,128)}, u32[]{:S(2)}) copy-start(s32[8,512]{1,0:T(8,128)} %near_ref.7) | copy-start | bytes 49156
  13.3 20.4 %all-to-all-start = ((f32[32,8,384]{2,1,0:T(8,128)}), f32[32,8,384]{2,1,0:T(8,128)S(1)}, u32[]{:S(2)}, u32[]{:S(2)}) async-start(f32[32,8,384]{2,1,0:T(8,128)} %bitcast.3), calls=%async_computation | async-start | bytes 786432 | tf_op jit(solution)/shard_map/all_to_all | solution.py:263
  23.6 0.7 %copy-start.5 = (f32[2,512]{1,0:T(2,128)S(1)}, f32[2,512]{1,0:T(2,128)}, u32[]{:S(2)}) copy-start(f32[2,512]{1,0:T(2,128)} %wind_ref.1) | copy-start | bytes 12292
  23.6 0.7 %copy-start.6 = (f32[512]{0:T(512)S(1)}, f32[512]{0:T(512)}, u32[]{:S(2)}) copy-start(f32[512]{0:T(512)} %param.10) | copy-start | bytes 6148
  37.2 14.8 %all-to-all-start.1 = ((f32[32,8,384]{2,1,0:T(8,128)}), f32[32,8,384]{2,1,0:T(8,128)S(1)}, u32[]{:S(2)}, u32[]{:S(2)}) async-start(f32[32,8,384]{2,1,0:T(8,128)} %bitcast.6), calls=%async_computation.1 | async-start | bytes 786432 | tf_op jit(solution)/shard_map/all_to_all | solution.py:263

commit v2 on v1

v2 whole, which is shorter than its diff:
```python
import math

import jax
import jax.numpy as jnp
import numpy as np
from jax import lax
from jax.experimental import pallas as pl
from jax.experimental.pallas import tpu as pltpu
from jax.sharding import PartitionSpec as P

NF = 36
ND = 36
K = 8
NP = 512
CAP = 8
N_MESH = 32
GHOSTS = N_MESH * CAP
BAND = 9
UP_REACH = 2
DOWN_REACH = 3
UP_SHIFT = 1
DOWN_SHIFT = 3
STRIDE = 40
ROWS = BAND * STRIDE + 8
LANES = 384

time_step = 0.5
group_scale = 0.8
quad_coupling = 0.25
wind_growth = 0.1
RATIOS = np.power(np.float64(1.1), np.arange(NF) - NF // 2)


def bf16_pieces(x):
    high = x.astype(jnp.bfloat16)
    low = (x - high.astype(jnp.float32)).astype(jnp.bfloat16)
    return jnp.concatenate([high, low], axis=0)


def exact_rows(c):
    high = c.astype(jnp.bfloat16).astype(jnp.float32)
    mid = (c - high).astype(jnp.bfloat16).astype(jnp.float32)
    return high + mid, (c - high) - mid


def by_band(band, values):
    picked = jnp.float32(values[3])
    for index in (2, 1, 0):
        picked = jnp.where(band == index, jnp.float32(values[index]), picked)
    return picked


def ratio_of(band, f):
    return by_band(band, [RATIOS[b * BAND + f] for b in range(NF // BAND)])


def scale_of(band, f):
    return by_band(band, [time_step * group_scale / RATIOS[b * BAND + f] for b in range(NF // BAND)])


def one_hot(entry_row, first, count):
    node = lax.broadcasted_iota(jnp.int32, (count, entry_row.shape[1]), 0) + first
    return jnp.where(node == entry_row, 1.0, 0.0).astype(jnp.bfloat16)


def gather(pieces, entry_row, first):
    got = jnp.dot(pieces, one_hot(entry_row, first, pieces.shape[1]), preferred_element_type=jnp.float32)
    return got[:ROWS] + got[ROWS:]


HALF = NP // 2
BOTTOM = BAND * STRIDE


def fill_rows(rows_ref, planes, cols):
    for f in range(BAND):
        rows_ref[f * STRIDE : f * STRIDE + ND, cols] = planes[f]


def packing_one_hot(send, count):
    slots = jnp.concatenate([send.astype(jnp.float32)] * N_MESH, axis=0)
    counts = jnp.broadcast_to(count.astype(jnp.float32), slots.shape)
    row = lax.broadcasted_iota(jnp.int32, slots.shape, 0)
    mine = lax.broadcasted_iota(jnp.int32, slots.shape, 1) == row // CAP
    node = jnp.sum(jnp.where(mine, slots, 0.0), axis=1, keepdims=True)
    used = jnp.sum(jnp.where(mine, counts, 0.0), axis=1, keepdims=True)
    place = lax.broadcasted_iota(jnp.int32, (GHOSTS, 1), 0) % CAP
    node = jnp.where(place.astype(jnp.float32) < used, node, -1.0).astype(jnp.int32)
    return jnp.where(lax.broadcasted_iota(jnp.int32, (GHOSTS, NP), 1) == node, 1.0, 0.0).astype(jnp.bfloat16)


def picked(hot, pieces):
    dims = (((1,), (1,)), ((), ()))
    return lax.dot_general(hot, pieces[:ROWS], dims, preferred_element_type=jnp.float32) + lax.dot_general(
        hot, pieces[ROWS:], dims, preferred_element_type=jnp.float32
    )


def wide(table, width):
    return jnp.concatenate([table] * (width // 128), axis=1)[:ND]


def delta(got, coords, axis):
    base = BOTTOM + 2 * axis
    return (got[base : base + 1] + got[base + 1 : base + 2]) - coords[axis : axis + 1]


def facing(cosine, sine, delta_x, delta_y):
    return jnp.maximum(-(cosine * delta_x + sine * delta_y), 0.0)


def rolled(x, shift):
    shift = shift % ND
    return jnp.concatenate([x[ND - shift :], x[: ND - shift]], axis=0)


def load_kernel(*refs):
    count = (len(refs) - 3) // 2
    sources, targets, sems = list(refs[:count]), refs[count:-1], refs[-1]
    sources += [
        sources[0].at[pl.ds(BAND - DOWN_REACH, DOWN_REACH)],
        sources[0].at[pl.ds(0, UP_REACH)],
    ]
    copies = [pltpu.make_async_copy(source, target, sems.at[i]) for i, (source, target) in enumerate(zip(sources, targets))]
    for copy in copies:
        copy.start()
    for copy in copies:
        copy.wait()


def spectra_pieces(spectra_ref, coords_ref, rows_ref):
    rows_ref[...] = jnp.zeros_like(rows_ref)
    for axis in range(2):
        first, second = exact_rows(coords_ref[axis : axis + 1, :])
        rows_ref[BOTTOM + 2 * axis : BOTTOM + 2 * axis + 1, :] = first
        rows_ref[BOTTOM + 2 * axis + 1 : BOTTOM + 2 * axis + 2, :] = second
    fill_rows(rows_ref, [spectra_ref[f] for f in range(BAND)], slice(None))
    return bf16_pieces(rows_ref[...])


def pack_kernel(spectra_ref, coords_ref, send_ref, count_ref, packed_ref, rows_ref):
    pieces = spectra_pieces(spectra_ref, coords_ref, rows_ref)
    packed_ref[:, :ROWS] = picked(packing_one_hot(send_ref[...], count_ref[...]), pieces)
    packed_ref[:, ROWS:] = jnp.zeros((GHOSTS, LANES - ROWS), jnp.float32)


def local_kernel(
    band_ref, spectra_ref, lower_ref, upper_ref, coords_ref, wind_ref, area_ref, near_ref, table_ref,
    base_ref, partial_ref, rows_ref,
):
    band = band_ref[0]
    pieces = spectra_pieces(spectra_ref, coords_ref, rows_ref)
    cosine, sine = wide(table_ref[0], NP), wide(table_ref[1], NP)
    for k in range(K):
        entry = near_ref[k : k + 1, :]
        got = gather(pieces, entry, 0)
        delta_x = jnp.where(entry < NP, delta(got, coords_ref[...], 0), 0.0)
        delta_y = jnp.where(entry < NP, delta(got, coords_ref[...], 1), 0.0)
        partial_ref[k, ND : ND + 1] = delta_x
        partial_ref[k, ND + 1 : ND + 2] = delta_y
        inflow = facing(cosine, sine, delta_x, delta_y)
        for f in range(BAND):
            term = inflow * got[f * STRIDE : f * STRIDE + ND]
            partial_ref[f, :ND] = term if k == 0 else partial_ref[f, :ND] + term
    partial_ref[K, ND : ND + 1] = area_ref[...]
    along = cosine * wind_ref[0:1, :] + sine * wind_ref[1:2, :]
    for f in range(BAND):
        density = spectra_ref[f]
        up = spectra_ref[f + UP_REACH] if f + UP_REACH < BAND else upper_ref[f + UP_REACH - BAND]
        down = spectra_ref[f - DOWN_REACH] if f >= DOWN_REACH else lower_ref[f]
        up_left, up_right = rolled(up, -UP_SHIFT), rolled(up, UP_SHIFT)
        down_left, down_right = rolled(down, DOWN_SHIFT), rolled(down, -DOWN_SHIFT)
        quad = quad_coupling * (
            density * density * (up_left + down_left + up_right + down_right)
            - 2.0 * density * (up_left * down_left + up_right * down_right)
        )
        growth = wind_growth * jnp.maximum(ratio_of(band, f) * along - 1.0, 0.0)
        base_ref[f] = density + time_step * (quad + growth * density)


def settle(band, f, base, area, total, weight):
    scaled = scale_of(band, f) * area
    return (base + scaled * total) / (1.0 + scaled * weight)


def ghost_pieces(ghost_ref):
    return bf16_pieces(ghost_ref[...].T[:ROWS])


def first_kernel(
    band_ref, ghost_ref, base_ref, partial_ref, coords_ref, near_ref, send_ref, count_ref, table_ref,
    packed_ref, pieces_ref, delta_ref, total_ref, rows_ref,
):
    band = band_ref[0]
    coords = coords_ref[...]
    pieces = ghost_pieces(ghost_ref)
    cosine, sine = wide(table_ref[0], NP), wide(table_ref[1], NP)
    weight = jnp.zeros((ND, NP), jnp.float32)
    for k in range(K):
        entry = near_ref[k : k + 1, :]
        got = gather(pieces, entry, NP)
        delta_x = jnp.where(entry < NP, partial_ref[k, ND : ND + 1], delta(got, coords, 0))
        delta_y = jnp.where(entry < NP, partial_ref[k, ND + 1 : ND + 2], delta(got, coords, 1))
        delta_ref[k : k + 1, :] = delta_x
        delta_ref[K + k : K + k + 1, :] = delta_y
        inflow = facing(cosine, sine, delta_x, delta_y)
        weight = weight + inflow
        for f in range(BAND):
            term = inflow * got[f * STRIDE : f * STRIDE + ND]
            total_ref[f] = (partial_ref[f, :ND] if k == 0 else total_ref[f]) + term
    area = partial_ref[K, ND : ND + 1]
    delta_ref[2 * K : 2 * K + 1, :] = area
    rows_ref[...] = jnp.zeros_like(rows_ref)
    fill_rows(rows_ref, [settle(band, f, base_ref[f], area, total_ref[f], weight) for f in range(BAND)], slice(None))
    current = bf16_pieces(rows_ref[...])
    pieces_ref[...] = current
    packed_ref[:, :ROWS] = picked(packing_one_hot(send_ref[...], count_ref[...]), current)
    packed_ref[:, ROWS:] = jnp.zeros((GHOSTS, LANES - ROWS), jnp.float32)


def second_local_kernel(pieces_ref, delta_ref, near_ref, table_ref, partial_ref):
    pieces = pieces_ref[...]
    cosine, sine = wide(table_ref[0], NP), wide(table_ref[1], NP)
    for k in range(K):
        got = gather(pieces, near_ref[k : k + 1, :], 0)
        inflow = facing(cosine, sine, delta_ref[k : k + 1, :], delta_ref[K + k : K + k + 1, :])
        for f in range(BAND):
            term = inflow * got[f * STRIDE : f * STRIDE + ND]
            partial_ref[f] = term if k == 0 else partial_ref[f] + term


def second_kernel(
    band_ref, ghost_ref, base_ref, partial_ref, delta_ref, near_ref, table_ref, out_ref, total_ref, sems
):
    band = band_ref[0]
    pieces = ghost_pieces(ghost_ref)
    cosine, sine = wide(table_ref[0], HALF), wide(table_ref[1], HALF)
    copies = []
    for half in range(2):
        cols = slice(half * HALF, (half + 1) * HALF)
        weight = jnp.zeros((ND, HALF), jnp.float32)
        for k in range(K):
            got = gather(pieces, near_ref[k : k + 1, cols], NP)
            inflow = facing(cosine, sine, delta_ref[k : k + 1, cols], delta_ref[K + k : K + k + 1, cols])
            weight = weight + inflow
            for f in range(BAND):
                term = inflow * got[f * STRIDE : f * STRIDE + ND]
                total_ref[f, :, cols] = (partial_ref[f, :, cols] if k == 0 else total_ref[f, :, cols]) + term
        area = delta_ref[2 * K : 2 * K + 1, cols]
        for f in range(BAND):
            total_ref[f, :, cols] = settle(band, f, base_ref[f, :, cols], area, total_ref[f, :, cols], weight)
        moved = pl.ds(half * HALF, HALF)
        copy = pltpu.make_async_copy(total_ref.at[:, :, moved], out_ref.at[:, :, moved], sems.at[half])
        copy.start()
        copies.append(copy)
    for copy in copies:
        copy.wait()


VMEM, SMEM, HBM = pltpu.VMEM, pltpu.SMEM, pltpu.HBM


def call(kernel, outs, scratch, name, *operands):
    return pl.pallas_call(
        kernel,
        out_shape=[jax.ShapeDtypeStruct(shape, dtype) for shape, dtype, _ in outs],
        in_specs=[pl.BlockSpec(memory_space=memory) for _, memory in operands],
        out_specs=[pl.BlockSpec(memory_space=memory) for _, _, memory in outs],
        scratch_shapes=scratch,
        compiler_params=pltpu.CompilerParams(vmem_limit_bytes=24 << 20),
        name=name,
        cost_estimate=pl.CostEstimate(flops=10**10, transcendentals=0, bytes_accessed=10**10),
    )(*[pltpu.with_memory_space_constraint(array, HBM) if memory is HBM else array for array, memory in operands])


def local(spectra, coords, inv_area, wind_vector, neighbours, send_nodes, send_count):
    bands = lax.axis_size("freq")
    band = lax.axis_index("freq").astype(jnp.int32).reshape(1)
    ends = bands - 1
    angles = (np.arange(STRIDE) + 0.5) * (2.0 * math.pi / ND)
    table = jnp.asarray(
        np.broadcast_to(np.stack([np.cos(angles), np.sin(angles)])[:, :, None], (2, STRIDE, 128)), jnp.float32
    )
    f32, planes = jnp.float32, (BAND, ND, NP)
    rows, dma = pltpu.VMEM((ROWS, NP), f32), pltpu.SemaphoreType.DMA
    split = ((2 * ROWS, NP), jnp.bfloat16, VMEM)

    def exchange(packed):
        packed = packed.reshape(N_MESH, CAP, LANES)
        return lax.all_to_all(packed, "mesh", split_axis=0, concat_axis=0, tiled=True).reshape(GHOSTS, LANES)

    def inside(*arrays):
        return [(array, VMEM) for array in arrays]

    inputs = (
        spectra, coords, wind_vector, inv_area.reshape(1, -1), neighbours,
        send_nodes.T, send_count.reshape(1, -1), table,
    )
    edges = [(DOWN_REACH, ND, NP), (UP_REACH, ND, NP)]
    spectra, coords, wind, area, near, send, count, table, tail, head = call(
        load_kernel,
        [(array.shape, array.dtype, VMEM) for array in inputs] + [(shape, f32, VMEM) for shape in edges],
        [dma((len(inputs) + 2,))],
        "load",
        *[(array, HBM) for array in inputs],
    )
    lower = lax.ppermute(tail, "freq", [(i, i + 1) for i in range(ends)])
    upper = lax.ppermute(head, "freq", [(i + 1, i) for i in range(ends)])
    (packed,) = call(
        pack_kernel, [((GHOSTS, LANES), f32, VMEM)], [rows], "pack", *inside(spectra, coords, send, count)
    )
    ghosts = exchange(packed)
    base, partial = call(
        local_kernel,
        [(planes, f32, VMEM), ((BAND, STRIDE, NP), f32, VMEM)],
        [rows],
        "local_first",
        (band, SMEM),
        *inside(spectra, lower, upper, coords, wind, area, near, table),
    )
    packed, pieces, deltas = call(
        first_kernel,
        [((GHOSTS, LANES), f32, VMEM), split, ((3 * K, NP), f32, VMEM)],
        [pltpu.VMEM(planes, f32), rows],
        "first",
        (band, SMEM),
        *inside(ghosts, base, partial, coords, near, send, count, table),
    )
    ghosts = exchange(packed)
    (partial,) = call(
        second_local_kernel, [(planes, f32, VMEM)], [], "local_second", *inside(pieces, deltas, near, table)
    )
    (updated,) = call(
        second_kernel,
        [(planes, f32, HBM)],
        [pltpu.VMEM(planes, f32), dma((2,))],
        "second",
        (band, SMEM),
        *inside(ghosts, base, partial, deltas, near, table),
    )
    return updated


def solution(mesh):
    in_specs = (
        P("freq", None, "mesh"),
        P(None, "mesh"),
        P("mesh"),
        P(None, "mesh"),
        P(None, "mesh"),
        P("mesh", None),
        P("mesh"),
    )
    out_specs = P("freq", None, "mesh")
    return jax.shard_map(local, mesh=mesh, in_specs=in_specs, out_specs=out_specs, check_vma=False)
```

time: 55.2 us -> 53.3 us (0.966)
  the two profiles are of different devices: /device:TPU:1 before, /device:TPU:0 now
where the time goes in v2:
time: 53.3 us; the launch traced here: 52.9 us
  starting transfers between devices  19.7 us (37%)
  Pallas kernels  16.7 us (31%)
  waiting for transfers between devices  16.5 us (31%)
    pallas_call x6, Pallas kernels, call(): pl.pallas_call(kernel, out_shape=[jax.ShapeDtypeStruct(shape, dtype) for...  16.7 us
    all_to_all x2, waiting for transfers between devices, exchange(): lax.all_to_all(packed, 'mesh', split_axis=0, concat_axis=0, tiled=True)  16.5 us
    all_to_all x2, starting transfers between devices, exchange(): lax.all_to_all(packed, 'mesh', split_axis=0, concat_axis=0, tiled=True)  15.4 us
    ppermute x1, starting transfers between devices, local(): lower = lax.ppermute(tail, 'freq', [(i, i + 1) for i in range(ends)])  3.05 us
    ppermute x1, starting transfers between devices, local(): upper = lax.ppermute(head, 'freq', [(i + 1, i) for i in range(ends)])  1.29 us
  transfers between devices with their start and end apart: 4, of which 2 were waited for; matrix products, arithmetic and copies ran while one was open for 0% of the time, Pallas kernels for 17%

profile of v2, /device:TPU:0, one launch (start us, length us, event | category | flops | bytes accessed | tf_op | source)
XLA Modules:
  0.0 52.9 jit_solution(2056523487560766497)
XLA Ops:
  0.0 1.4 %load.1 = (f32[9,36,512]{2,1,0:T(8,128)S(1)}, f32[2,512]{1,0:T(2,128)S(1)}, f32[2,512]{1,0:T(2,128)S(1)}, f32[1,512]{1,0:T(1,128)S(1)}, s32[8,512]{1,0:T(8,128)S...) custom-call(f32[9,36,512]{2,1,0:T(8,128)} %refs_0_.1, ...), custom_call_target="tpu_custom_call" | custom-call | flops 10000000000 | bytes 10000000000 | tf_op jit(solution)/shard_map/load/pallas_call | solution.py:264
  1.4 1.3 %collective-permute-start.1 = (f32[2,36,512]{2,1,0:T(8,128)S(1)}, f32[2,36,512]{2,1,0:T(8,128)S(1)}, u32[]{:S(2)}, u32[]{:S(2)}) collective-permute-start(f32[2,36,512]{2,1,0:T(8,128)S(1)} %get-tuple-element.25), channel_id=1, source_target_pairs={{1,0},{2,1},{3,2},{5,4},{6,5},{7,6},{9,8},{10,9},{11,10},{13,12},{... | collective-permute-start | bytes 442376 | tf_op jit(solution)/shard_map/ppermute | solution.py:308
  2.7 3.0 %collective-permute-start = (f32[3,36,512]{2,1,0:T(8,128)S(1)}, f32[3,36,512]{2,1,0:T(8,128)S(1)}, u32[]{:S(2)}, u32[]{:S(2)}) collective-permute-start(f32[3,36,512]{2,1,0:T(8,128)S(1)} %get-tuple-element.24), channel_id=1, source_target_pairs={{0,1},{1,2},{2,3},{4,5},{5,6},{6,7},{8,9},{9,10},{10,11},{12,13},{... | collective-permute-start | bytes 663560 | tf_op jit(solution)/shard_map/ppermute | solution.py:307
  5.8 1.3 %pack.1 = f32[256,384]{1,0:T(8,128)} custom-call(f32[9,36,512]{2,1,0:T(8,128)S(1)} %get-tuple-element.20.spectra_ref, f32[2,512]{1,0:T(2,128)S(1)} %get-tuple-element.21.coords_ref, s32[8,32]{1,0:T(8,128)S(1)} %get-tuple-element.22.send_ref, s32[1,32]{1,0:T(1,128)S(1)} %get-tuple-element.23.count_ref), custom_call_target="tpu_custom_call" | custom-call | flops 10000000000 | bytes 10000000000 | tf_op jit(solution)/shard_map/pack/pallas_call | solution.py:264
  7.0 10.9 %all-to-all-start = ((f32[32,8,384]{2,1,0:T(8,128)}), f32[32,8,384]{2,1,0:T(8,128)S(1)}, u32[]{:S(2)}, u32[]{:S(2)}) async-start(f32[32,8,384]{2,1,0:T(8,128)} %bitcast.4), calls=%async_computation | async-start | bytes 786432 | tf_op jit(solution)/shard_map/all_to_all | solution.py:290
  17.9 0.0 collective-permute-done.1.upper_ref
  17.9 0.0 collective-permute-done.lower_ref
  18.0 4.5 %local_first.1 = (f32[9,36,512]{2,1,0:T(8,128)S(1)}, f32[9,40,512]{2,1,0:T(8,128)S(1)}) custom-call(s32[1]{0:T(128)} %bitcast.band_ref, f32[9,36,512]{2,1,0:T(8,128)S(1)} %get-tuple-element.20.spectra_ref, f32[3,36,512]{2,1,0:T(8,128)S(1)} %collective-permute-done.lower_ref, f32[2,36,512]{2,1,0:T(8,128)S(1)} %collective-permute-done.1.upper_ref, ...), custom_call_target="tpu_custom_call" | custom-call | flops 10000000000 | bytes 10000000000 | tf_op jit(solution)/shard_map/local_first/pallas_call | solution.py:264
  22.4 8.2 %all-to-all-done = f32[32,8,384]{2,1,0:T(8,128)S(1)} async-done(((f32[32,8,384]{2,1,0:T(8,128)}), f32[32,8,384]{2,1,0:T(8,128)S(1)}, u32[]{:S(2)}, u32[]{:S(2)}) %all-to-all-start) | async-done | bytes 393248 | tf_op jit(solution)/shard_map/all_to_all | solution.py:290
  30.6 3.5 %first.1 = (f32[256,384]{1,0:T(8,128)}, bf16[736,512]{1,0:T(8,128)(2,1)S(1)}, f32[24,512]{1,0:T(8,128)S(1)}) custom-call(s32[1]{0:T(128)} %bitcast.band_ref, f32[256,384]{1,0:T(8,128)S(1)} %bitcast.8, f32[9,36,512]{2,1,0:T(8,128)S(1)} %get-tuple-element.30.base_ref, f32[9,40,512]{2,1,0:T(8,128)S(1)} %get-tuple-element.31.partial_ref, ...), custom_call_target="tpu_custom_call" | custom-call | flops 10000000000 | bytes 10000000000 | tf_op jit(solution)/shard_map/first/pallas_call | solution.py:264
  34.1 4.5 %all-to-all-start.1 = ((f32[32,8,384]{2,1,0:T(8,128)}), f32[32,8,384]{2,1,0:T(8,128)S(1)}, u32[]{:S(2)}, u32[]{:S(2)}) async-start(f32[32,8,384]{2,1,0:T(8,128)} %bitcast.6), calls=%async_computation.1 | async-start | bytes 786432 | tf_op jit(solution)/shard_map/all_to_all | solution.py:290
  38.6 3.3 %local_second.1.partial_ref = f32[9,36,512]{2,1,0:T(8,128)S(1)} custom-call(bf16[736,512]{1,0:T(8,128)(2,1)S(1)} %get-tuple-element.33.pieces_ref, f32[24,512]{1,0:T(8,128)S(1)} %get-tuple-element.34.delta_ref, s32[8,512]{1,0:T(8,128)S(1)} %get-tuple-element.28.near_ref, f32[2,40,128]{2,1,0:T(8,128)S(1)} %get-tuple-element.29.table_ref), custom_call_target="tpu_custom_call" | custom-call | flops 10000000000 | bytes 10000000000 | tf_op jit(solution)/shard_map/local_second/pallas_call | solution.py:264
  41.9 8.3 %all-to-all-done.1 = f32[32,8,384]{2,1,0:T(8,128)S(1)} async-done(((f32[32,8,384]{2,1,0:T(8,128)}), f32[32,8,384]{2,1,0:T(8,128)S(1)}, u32[]{:S(2)}, u32[]{:S(2)}) %all-to-all-start.1) | async-done | bytes 393248 | tf_op jit(solution)/shard_map/all_to_all | solution.py:290
  50.2 2.7 %second.1 = f32[9,36,512]{2,1,0:T(8,128)} custom-call(s32[1]{0:T(128)} %bitcast.band_ref, f32[256,384]{1,0:T(8,128)S(1)} %bitcast.9, f32[9,36,512]{2,1,0:T(8,128)S(1)} %get-tuple-element.30.base_ref, f32[9,36,512]{2,1,0:T(8,128)S(1)} %local_second.1.partial_ref, f32[24,512]{1,0:T(8,128)S(1)} %get-tuple-element.34.delta_ref, ...), custom_call_target="tpu_custom_call" | custom-call | flops 10000000000 | bytes 10000000000 | tf_op jit(solution)/shard_map/second/pallas_call | solution.py:264
Async XLA Ops:
  1.4 16.5 %collective-permute-start.1 = (f32[2,36,512]{2,1,0:T(8,128)S(1)}, f32[2,36,512]{2,1,0:T(8,128)S(1)}, u32[]{:S(2)}, u32[]{:S(2)}) collective-permute-start(f32[2,36,512]{2,1,0:T(8,128)S(1)} %get-tuple-element.25), channel_id=1, source_target_pairs={{1,0},{2,1},{3,2},{5,4},{6,5},{7,6},{9,8},{10,9},{11,10},{13,12},{... | collective-permute-start | bytes 442376 | tf_op jit(solution)/shard_map/ppermute | solution.py:308
  2.7 15.2 %collective-permute-start = (f32[3,36,512]{2,1,0:T(8,128)S(1)}, f32[3,36,512]{2,1,0:T(8,128)S(1)}, u32[]{:S(2)}, u32[]{:S(2)}) collective-permute-start(f32[3,36,512]{2,1,0:T(8,128)S(1)} %get-tuple-element.24), channel_id=1, source_target_pairs={{0,1},{1,2},{2,3},{4,5},{5,6},{6,7},{8,9},{9,10},{10,11},{12,13},{... | collective-permute-start | bytes 663560 | tf_op jit(solution)/shard_map/ppermute | solution.py:307
  7.0 23.5 %all-to-all-start = ((f32[32,8,384]{2,1,0:T(8,128)}), f32[32,8,384]{2,1,0:T(8,128)S(1)}, u32[]{:S(2)}, u32[]{:S(2)}) async-start(f32[32,8,384]{2,1,0:T(8,128)} %bitcast.4), calls=%async_computation | async-start | bytes 786432 | tf_op jit(solution)/shard_map/all_to_all | solution.py:290
  34.1 16.1 %all-to-all-start.1 = ((f32[32,8,384]{2,1,0:T(8,128)}), f32[32,8,384]{2,1,0:T(8,128)S(1)}, u32[]{:S(2)}, u32[]{:S(2)}) async-start(f32[32,8,384]{2,1,0:T(8,128)} %bitcast.6), calls=%async_computation.1 | async-start | bytes 786432 | tf_op jit(solution)/shard_map/all_to_all | solution.py:290

commit v3 on v2

v3 whole, which is shorter than its diff:
```python
import math

import jax
import jax.numpy as jnp
import numpy as np
from jax import lax
from jax.experimental import pallas as pl
from jax.experimental.pallas import tpu as pltpu
from jax.sharding import PartitionSpec as P

NF = 36
ND = 36
K = 8
NP = 512
CAP = 8
N_MESH = 32
GHOSTS = N_MESH * CAP
BAND = 9
UP_REACH = 2
DOWN_REACH = 3
UP_SHIFT = 1
DOWN_SHIFT = 3
COORDS = BAND * ND
ROWS = COORDS + 4
LANES = 384
PAIR = 2 * ND
GROUPS = [(0, PAIR), (PAIR, PAIR), (2 * PAIR, PAIR), (3 * PAIR, PAIR), (4 * PAIR, ROWS - 4 * PAIR)]

time_step = 0.5
group_scale = 0.8
quad_coupling = 0.25
wind_growth = 0.1
RATIOS = np.power(np.float64(1.1), np.arange(NF) - NF // 2)


def rounded(x):
    return x.astype(jnp.bfloat16).astype(jnp.float32)


def bf16_pieces(x):
    high = rounded(x)
    return jnp.concatenate([high, x - high], axis=0).astype(jnp.bfloat16)


def exact_rows(c):
    high = rounded(c)
    mid = rounded(c - high)
    return high + mid, (c - high) - mid


def by_band(band, values):
    picked = jnp.float32(values[3])
    for index in (2, 1, 0):
        picked = jnp.where(band == index, jnp.float32(values[index]), picked)
    return picked


def ratio_of(band, f):
    return by_band(band, [RATIOS[b * BAND + f] for b in range(NF // BAND)])


def scale_of(band, f):
    return by_band(band, [time_step * group_scale / RATIOS[b * BAND + f] for b in range(NF // BAND)])


def one_hot(entry_row, first, count):
    node = lax.broadcasted_iota(jnp.int32, (count, entry_row.shape[1]), 0) + first
    return jnp.where(node == entry_row, 1.0, 0.0).astype(jnp.bfloat16)


def gather(pieces, entry_row, first):
    got = jnp.dot(pieces, one_hot(entry_row, first, pieces.shape[1]), preferred_element_type=jnp.float32)
    return got[:ROWS] + got[ROWS:]


def fill_coords(rows_ref, coords_ref):
    for axis in range(2):
        first, second = exact_rows(coords_ref[axis : axis + 1, :])
        rows_ref[COORDS + 2 * axis : COORDS + 2 * axis + 1, :] = first
        rows_ref[COORDS + 2 * axis + 1 : COORDS + 2 * axis + 2, :] = second


def fill_rows(rows_ref, spectra_ref, coords_ref):
    for f in range(BAND):
        rows_ref[f * ND : (f + 1) * ND, :] = spectra_ref[f]
    fill_coords(rows_ref, coords_ref)


def packing_one_hot(send, count):
    slots = jnp.concatenate([send.astype(jnp.float32)] * N_MESH, axis=0)
    counts = jnp.broadcast_to(count.astype(jnp.float32), slots.shape)
    row = lax.broadcasted_iota(jnp.int32, slots.shape, 0)
    mine = lax.broadcasted_iota(jnp.int32, slots.shape, 1) == row // CAP
    node = jnp.sum(jnp.where(mine, slots, 0.0), axis=1, keepdims=True)
    used = jnp.sum(jnp.where(mine, counts, 0.0), axis=1, keepdims=True)
    place = lax.broadcasted_iota(jnp.int32, (GHOSTS, 1), 0) % CAP
    node = jnp.where(place.astype(jnp.float32) < used, node, -1.0).astype(jnp.int32)
    return jnp.where(lax.broadcasted_iota(jnp.int32, (GHOSTS, NP), 1) == node, 1.0, 0.0).astype(jnp.bfloat16)


def pack(rows, send_ref, count_ref, packed_ref):
    hot = packing_one_hot(send_ref[...], count_ref[...])
    high = rows.astype(jnp.bfloat16)
    low = (rows - high.astype(jnp.float32)).astype(jnp.bfloat16)
    dims = (((1,), (1,)), ((), ()))
    packed_ref[:, :ROWS] = lax.dot_general(hot, high, dims, preferred_element_type=jnp.float32) + lax.dot_general(
        hot, low, dims, preferred_element_type=jnp.float32
    )
    packed_ref[:, ROWS:] = jnp.zeros((GHOSTS, LANES - ROWS), jnp.float32)


def directions():
    place = lax.broadcasted_iota(jnp.int32, (8, 128), 0)
    within = [jnp.full((8, 128), 0.0, jnp.float32)] * 2
    for row in range(8):
        angle = (row + 0.5) * 2.0 * math.pi / ND
        within = [jnp.where(place == row, jnp.float32(g(angle)), old) for g, old in zip((math.cos, math.sin), within)]
    inner_cosine, inner_sine = within
    cosine, sine = [], []
    for tile in range(PAIR // 8):
        angle = 8 * tile * 2.0 * math.pi / ND
        outer_cosine, outer_sine = jnp.float32(math.cos(angle)), jnp.float32(math.sin(angle))
        cosine.append(outer_cosine * inner_cosine - outer_sine * inner_sine)
        sine.append(outer_sine * inner_cosine + outer_cosine * inner_sine)
    return [jnp.concatenate([jnp.concatenate(tiles, axis=0)] * (NP // 128), axis=1) for tiles in (cosine, sine)]


def delta(got, coords, axis):
    row = COORDS + 2 * axis
    return (got[row : row + 1] + got[row + 1 : row + 2]) - coords[axis : axis + 1]


def facing(cosine, sine, delta_x, delta_y):
    return jnp.maximum(-(cosine * delta_x + sine * delta_y), 0.0)


def add_slot(target_ref, source_ref, inflow, got, fresh):
    for start, size in GROUPS:
        rows = slice(start, start + size)
        term = inflow[:size] * got[rows]
        target_ref[rows] = term if fresh else source_ref[rows] + term


def rolled(x, shift):
    shift = shift % ND
    return jnp.concatenate([x[ND - shift :], x[: ND - shift]], axis=0)


def pack_kernel(
    band_ref, spectra_hbm, coords_hbm, send_hbm, count_hbm, wind_hbm, area_hbm, near_hbm,
    packed_ref, spectra_ref, coords_ref, send_ref, count_ref, wind_ref, area_ref, near_ref, near_edge_ref, far_edge_ref,
    rows_ref, sems,
):
    odd = lax.rem(band_ref[0], 2)
    inner = pl.ds((1 - odd) * (BAND - DOWN_REACH), DOWN_REACH)
    outer = pl.ds(odd * (BAND - DOWN_REACH), DOWN_REACH)
    pairs = (
        (spectra_hbm, spectra_ref),
        (coords_hbm, coords_ref),
        (send_hbm, send_ref),
        (count_hbm, count_ref),
        (spectra_hbm.at[inner], near_edge_ref),
        (spectra_hbm.at[outer], far_edge_ref),
        (wind_hbm, wind_ref),
        (area_hbm, area_ref),
        (near_hbm, near_ref),
    )
    copies = [pltpu.make_async_copy(source, target, sems.at[i]) for i, (source, target) in enumerate(pairs)]
    for copy in copies:
        copy.start()
    for copy in copies[:4]:
        copy.wait()
    fill_rows(rows_ref, spectra_ref, coords_ref)
    pack(rows_ref[...], send_ref, count_ref, packed_ref)
    for copy in copies[4:]:
        copy.wait()


def local_kernel(
    band_ref, spectra_ref, near_edge_ref, far_edge_ref, coords_ref, wind_ref, area_ref, near_ref,
    base_ref, partial_ref, rows_ref,
):
    band = band_ref[0]
    coords = coords_ref[...]
    fill_rows(rows_ref, spectra_ref, coords_ref)
    pieces = bf16_pieces(rows_ref[...])
    cosine, sine = directions()
    for k in range(K):
        entry = near_ref[k : k + 1, :]
        got = gather(pieces, entry, 0)
        delta_x = jnp.where(entry < NP, delta(got, coords, 0), 0.0)
        delta_y = jnp.where(entry < NP, delta(got, coords, 1), 0.0)
        partial_ref[ROWS + k : ROWS + k + 1] = delta_x
        partial_ref[ROWS + K + k : ROWS + K + k + 1] = delta_y
        add_slot(partial_ref, partial_ref, facing(cosine, sine, delta_x, delta_y), got, k == 0)
    partial_ref[ROWS + 2 * K : ROWS + 2 * K + 1] = area_ref[...]
    along = cosine[:ND] * wind_ref[0:1, :] + sine[:ND] * wind_ref[1:2, :]
    odd = lax.rem(band, 2) == 1
    lower = [jnp.where(odd, near_edge_ref[f], far_edge_ref[f]) for f in range(DOWN_REACH)]
    upper = [jnp.where(odd, far_edge_ref[f], near_edge_ref[f]) for f in range(UP_REACH)]
    base_ref[COORDS:] = jnp.zeros((ROWS - COORDS, NP), jnp.float32)
    for f in range(BAND):
        density = spectra_ref[f]
        up = spectra_ref[f + UP_REACH] if f + UP_REACH < BAND else upper[f + UP_REACH - BAND]
        down = spectra_ref[f - DOWN_REACH] if f >= DOWN_REACH else lower[f]
        up_left, up_right = rolled(up, -UP_SHIFT), rolled(up, UP_SHIFT)
        down_left, down_right = rolled(down, DOWN_SHIFT), rolled(down, -DOWN_SHIFT)
        quad = quad_coupling * (
            density * density * (up_left + down_left + up_right + down_right)
            - 2.0 * density * (up_left * down_left + up_right * down_right)
        )
        growth = wind_growth * jnp.maximum(ratio_of(band, f) * along - 1.0, 0.0)
        base_ref[f * ND : (f + 1) * ND] = density + time_step * (quad + growth * density)


def settle(band, base_ref, area, total_ref, weight, group, target_ref):
    start, size = group
    rows = slice(start, start + size)
    lower, upper = start // ND, min(start // ND + 1, BAND - 1)
    row = lax.broadcasted_iota(jnp.int32, (size, NP), 0)
    scaled = jnp.where(row < ND, scale_of(band, lower), scale_of(band, upper)) * area
    target_ref[rows] = (base_ref[rows] + scaled * total_ref[rows]) / (1.0 + scaled * weight[:size])


def ghost_pieces(ghost_ref):
    return bf16_pieces(ghost_ref[...].T[:ROWS])


def first_kernel(
    band_ref, ghost_ref, base_ref, partial_ref, coords_ref, near_ref, send_ref, count_ref,
    packed_ref, total_ref, delta_ref,
):
    band = band_ref[0]
    coords = coords_ref[...]
    pieces = ghost_pieces(ghost_ref)
    cosine, sine = directions()
    weight = jnp.zeros((PAIR, NP), jnp.float32)
    for k in range(K):
        entry = near_ref[k : k + 1, :]
        got = gather(pieces, entry, NP)
        delta_x = jnp.where(entry < NP, partial_ref[ROWS + k : ROWS + k + 1], delta(got, coords, 0))
        delta_y = jnp.where(entry < NP, partial_ref[ROWS + K + k : ROWS + K + k + 1], delta(got, coords, 1))
        delta_ref[k : k + 1, :] = delta_x
        delta_ref[K + k : K + k + 1, :] = delta_y
        inflow = facing(cosine, sine, delta_x, delta_y)
        weight = weight + inflow
        add_slot(total_ref, partial_ref if k == 0 else total_ref, inflow, got, False)
    area = partial_ref[ROWS + 2 * K : ROWS + 2 * K + 1]
    delta_ref[2 * K : 2 * K + 1, :] = area
    for group in GROUPS:
        settle(band, base_ref, area, total_ref, weight, group, total_ref)
    pack(total_ref[...], send_ref, count_ref, packed_ref)


def second_local_kernel(current_ref, delta_ref, near_ref, partial_ref):
    pieces = bf16_pieces(current_ref[...])
    cosine, sine = directions()
    for k in range(K):
        got = gather(pieces, near_ref[k : k + 1, :], 0)
        inflow = facing(cosine, sine, delta_ref[k : k + 1, :], delta_ref[K + k : K + k + 1, :])
        add_slot(partial_ref, partial_ref, inflow, got, k == 0)


def second_kernel(
    band_ref, ghost_ref, base_ref, partial_ref, delta_ref, near_ref, out_ref, total_ref, planes_ref, sems
):
    band = band_ref[0]
    pieces = ghost_pieces(ghost_ref)
    cosine, sine = directions()
    weight = jnp.zeros((PAIR, NP), jnp.float32)
    for k in range(K):
        got = gather(pieces, near_ref[k : k + 1, :], NP)
        inflow = facing(cosine, sine, delta_ref[k : k + 1, :], delta_ref[K + k : K + k + 1, :])
        weight = weight + inflow
        add_slot(total_ref, partial_ref if k == 0 else total_ref, inflow, got, False)
    area = delta_ref[2 * K : 2 * K + 1, :]
    copies = []
    for index, group in enumerate(GROUPS):
        settle(band, base_ref, area, total_ref, weight, group, total_ref)
        first = 2 * index
        count = min(2, BAND - first)
        for f in range(first, first + count):
            planes_ref[f] = total_ref[f * ND : (f + 1) * ND]
        moved = pl.ds(first, count)
        copies.append(pltpu.make_async_copy(planes_ref.at[moved], out_ref.at[moved], sems.at[index]))
        copies[-1].start()
    for copy in copies:
        copy.wait()


VMEM, SMEM, HBM = pltpu.VMEM, pltpu.SMEM, pltpu.HBM


def call(kernel, outs, scratch, name, *operands):
    return pl.pallas_call(
        kernel,
        out_shape=[jax.ShapeDtypeStruct(shape, dtype) for shape, dtype, _ in outs],
        in_specs=[pl.BlockSpec(memory_space=memory) for _, memory in operands],
        out_specs=[pl.BlockSpec(memory_space=memory) for _, _, memory in outs],
        scratch_shapes=scratch,
        compiler_params=pltpu.CompilerParams(vmem_limit_bytes=24 << 20),
        name=name,
        cost_estimate=pl.CostEstimate(flops=10**10, transcendentals=0, bytes_accessed=10**10),
    )(*[pltpu.with_memory_space_constraint(array, HBM) if memory is HBM else array for array, memory in operands])


def local(spectra, coords, inv_area, wind_vector, neighbours, send_nodes, send_count):
    bands = lax.axis_size("freq")
    band = lax.axis_index("freq").astype(jnp.int32).reshape(1)
    f32, planes = jnp.float32, (BAND, ND, NP)
    rows, dma = pltpu.VMEM((ROWS, NP), f32), pltpu.SemaphoreType.DMA
    send, count, area = send_nodes.T, send_count.reshape(1, -1), inv_area.reshape(1, -1)

    def exchange(packed):
        packed = packed.reshape(N_MESH, CAP, LANES)
        return lax.all_to_all(packed, "mesh", split_axis=0, concat_axis=0, tiled=True).reshape(GHOSTS, LANES)

    def inside(*arrays):
        return [(array, VMEM) for array in arrays]

    inputs = (spectra, coords, send, count, wind_vector, area, neighbours)
    packed, spectra, coords, send, count, wind, area, near, near_edge, far_edge = call(
        pack_kernel,
        [((GHOSTS, LANES), f32, VMEM)]
        + [(array.shape, array.dtype, VMEM) for array in inputs]
        + [((DOWN_REACH, ND, NP), f32, VMEM)] * 2,
        [rows, dma((len(inputs) + 2,))],
        "pack",
        (band, SMEM),
        *[(array, HBM) for array in inputs],
    )
    pairs = [[pair for i in range(start, bands - 1, 2) for pair in ((i, i + 1), (i + 1, i))] for start in (0, 1)]
    near_edge = lax.ppermute(near_edge, "freq", pairs[0])
    far_edge = lax.ppermute(far_edge, "freq", pairs[1])
    ghosts = exchange(packed)
    base, partial = call(
        local_kernel,
        [((ROWS, NP), f32, VMEM), ((ROWS + 3 * K, NP), f32, VMEM)],
        [rows],
        "local_first",
        (band, SMEM),
        *inside(spectra, near_edge, far_edge, coords, wind, area, near),
    )
    packed, current, deltas = call(
        first_kernel,
        [((GHOSTS, LANES), f32, VMEM), ((ROWS, NP), f32, VMEM), ((3 * K, NP), f32, VMEM)],
        [],
        "first",
        (band, SMEM),
        *inside(ghosts, base, partial, coords, near, send, count),
    )
    ghosts = exchange(packed)
    (partial,) = call(
        second_local_kernel, [((ROWS, NP), f32, VMEM)], [], "local_second", *inside(current, deltas, near)
    )
    (updated,) = call(
        second_kernel,
        [(planes, f32, HBM)],
        [rows, pltpu.VMEM(planes, f32), dma((len(GROUPS),))],
        "second",
        (band, SMEM),
        *inside(ghosts, base, partial, deltas, near),
    )
    return updated


def solution(mesh):
    in_specs = (
        P("freq", None, "mesh"),
        P(None, "mesh"),
        P("mesh"),
        P(None, "mesh"),
        P(None, "mesh"),
        P("mesh", None),
        P("mesh"),
    )
    out_specs = P("freq", None, "mesh")
    return jax.shard_map(local, mesh=mesh, in_specs=in_specs, out_specs=out_specs, check_vma=False)
```

time: 53.3 us -> 50 us (0.938)
  the two profiles are of different devices: /device:TPU:0 before, /device:TPU:1 now
where the time goes in v3:
time: 50 us; the launch traced here: 49.7 us
  starting transfers between devices  19 us (38%)
  Pallas kernels  16 us (32%)
  waiting for transfers between devices  14.4 us (29%)
    pallas_call x5, Pallas kernels, call(): pl.pallas_call(kernel, out_shape=[jax.ShapeDtypeStruct(shape, dtype) for...  16 us
    all_to_all x2, waiting for transfers between devices, exchange(): lax.all_to_all(packed, 'mesh', split_axis=0, concat_axis=0, tiled=True)  14.4 us
    all_to_all x2, starting transfers between devices, exchange(): lax.all_to_all(packed, 'mesh', split_axis=0, concat_axis=0, tiled=True)  14.3 us
    ppermute x1, starting transfers between devices, local(): far_edge = lax.ppermute(far_edge, 'freq', pairs[1])  3.19 us
    ppermute x1, starting transfers between devices, local(): near_edge = lax.ppermute(near_edge, 'freq', pairs[0])  1.5 us
  transfers between devices with their start and end apart: 4, of which 2 were waited for; matrix products, arithmetic and copies ran while one was open for 0% of the time, Pallas kernels for 16%

profile of v3, /device:TPU:1, one launch (start us, length us, event | category | flops | bytes accessed | tf_op | source)
XLA Modules:
  0.0 49.7 jit_solution(11816120391457043166)
XLA Ops:
  0.0 2.5 %pack.1 = (f32[256,384]{1,0:T(8,128)}, f32[9,36,512]{2,1,0:T(8,128)S(1)}, f32[2,512]{1,0:T(2,128)S(1)}, s32[8,32]{1,0:T(8,128)S(1)}, s32[1,32]{1,0:T(1,128)S(1)}...) custom-call(s32[1]{0:T(128)} %bitcast.band_ref, ...), custom_call_target="tpu_custom_call" | custom-call | flops 10000000000 | bytes 10000000000 | tf_op jit(solution)/shard_map/pack/pallas_call | solution.py:295
  2.5 1.5 %collective-permute-start = (f32[3,36,512]{2,1,0:T(8,128)S(1)}, f32[3,36,512]{2,1,0:T(8,128)S(1)}, u32[]{:S(2)}, u32[]{:S(2)}) collective-permute-start(f32[3,36,512]{2,1,0:T(8,128)S(1)} %get-tuple-element.22), channel_id=1, source_target_pairs={{0,1},{1,0},{2,3},{3,2},{4,5},{5,4},{6,7},{7,6},{8,9},{9,8},{10,11... | collective-permute-start | bytes 663560 | tf_op jit(solution)/shard_map/ppermute | solution.py:333
  4.0 3.2 %collective-permute-start.1 = (f32[3,36,512]{2,1,0:T(8,128)S(1)}, f32[3,36,512]{2,1,0:T(8,128)S(1)}, u32[]{:S(2)}, u32[]{:S(2)}) collective-permute-start(f32[3,36,512]{2,1,0:T(8,128)S(1)} %get-tuple-element.23), channel_id=1, source_target_pairs={{1,2},{2,1},{5,6},{6,5},{9,10},{10,9},{13,14},{14,13},{17,18},{18,... | collective-permute-start | bytes 663560 | tf_op jit(solution)/shard_map/ppermute | solution.py:334
  7.2 10.2 %all-to-all-start = ((f32[32,8,384]{2,1,0:T(8,128)}), f32[32,8,384]{2,1,0:T(8,128)S(1)}, u32[]{:S(2)}, u32[]{:S(2)}) async-start(f32[32,8,384]{2,1,0:T(8,128)} %bitcast.4), calls=%async_computation | async-start | bytes 786432 | tf_op jit(solution)/shard_map/all_to_all | solution.py:316
  17.4 0.0 collective-permute-done.near_edge_ref
  17.5 0.0 collective-permute-done.1.far_edge_ref
  17.5 4.6 %local_first.1 = (f32[328,512]{1,0:T(8,128)S(1)}, f32[352,512]{1,0:T(8,128)S(1)}) custom-call(s32[1]{0:T(128)} %bitcast.band_ref, f32[9,36,512]{2,1,0:T(8,128)S(1)} %get-tuple-element.21.spectra_ref, f32[3,36,512]{2,1,0:T(8,128)S(1)} %collective-permute-done.near_edge_ref, f32[3,36,512]{2,1,0:T(8,128)S(1)} %collective-permute-done.1.far_edge_ref, ...), custom_call_target="tpu_custom_call" | custom-call | flops 10000000000 | bytes 10000000000 | tf_op jit(solution)/shard_map/local_first/pallas_call | solution.py:295
  22.1 6.2 %all-to-all-done = f32[32,8,384]{2,1,0:T(8,128)S(1)} async-done(((f32[32,8,384]{2,1,0:T(8,128)}), f32[32,8,384]{2,1,0:T(8,128)S(1)}, u32[]{:S(2)}, u32[]{:S(2)}) %all-to-all-start) | async-done | bytes 393248 | tf_op jit(solution)/shard_map/all_to_all | solution.py:316
  28.2 3.3 %first.1 = (f32[256,384]{1,0:T(8,128)}, f32[328,512]{1,0:T(8,128)S(1)}, f32[24,512]{1,0:T(8,128)S(1)}) custom-call(s32[1]{0:T(128)} %bitcast.band_ref, f32[256,384]{1,0:T(8,128)S(1)} %bitcast.8, f32[328,512]{1,0:T(8,128)S(1)} %get-tuple-element.28.base_ref, f32[352,512]{1,0:T(8,128)S(1)} %get-tuple-element.29.partial_ref, ...), custom_call_target="tpu_custom_call" | custom-call | flops 10000000000 | bytes 10000000000 | tf_op jit(solution)/shard_map/first/pallas_call | solution.py:295
  31.5 4.1 %all-to-all-start.1 = ((f32[32,8,384]{2,1,0:T(8,128)}), f32[32,8,384]{2,1,0:T(8,128)S(1)}, u32[]{:S(2)}, u32[]{:S(2)}) async-start(f32[32,8,384]{2,1,0:T(8,128)} %bitcast.6), calls=%async_computation.1 | async-start | bytes 786432 | tf_op jit(solution)/shard_map/all_to_all | solution.py:316
  35.6 3.1 %local_second.1.partial_ref = f32[328,512]{1,0:T(8,128)S(1)} custom-call(f32[328,512]{1,0:T(8,128)S(1)} %get-tuple-element.33.current_ref, f32[24,512]{1,0:T(8,128)S(1)} %get-tuple-element.34.delta_ref, s32[8,512]{1,0:T(8,128)S(1)} %get-tuple-element.27.near_ref), custom_call_target="tpu_custom_call" | custom-call | flops 10000000000 | bytes 10000000000 | tf_op jit(solution)/shard_map/local_second/pallas_call | solution.py:295
  38.7 8.3 %all-to-all-done.1 = f32[32,8,384]{2,1,0:T(8,128)S(1)} async-done(((f32[32,8,384]{2,1,0:T(8,128)}), f32[32,8,384]{2,1,0:T(8,128)S(1)}, u32[]{:S(2)}, u32[]{:S(2)}) %all-to-all-start.1) | async-done | bytes 393248 | tf_op jit(solution)/shard_map/all_to_all | solution.py:316
  47.0 2.5 %second.1 = f32[9,36,512]{2,1,0:T(8,128)} custom-call(s32[1]{0:T(128)} %bitcast.band_ref, f32[256,384]{1,0:T(8,128)S(1)} %bitcast.9, f32[328,512]{1,0:T(8,128)S(1)} %get-tuple-element.28.base_ref, f32[328,512]{1,0:T(8,128)S(1)} %local_second.1.partial_ref, f32[24,512]{1,0:T(8,128)S(1)} %get-tuple-element.34.delta_ref, s32[8,512]{1,0:T(8,128)S(1)} %get-tuple-element.27.near_ref), custom_call_target="tpu_custom_call" | custom-call | flops 10000000000 | bytes 10000000000 | tf_op jit(solution)/shard_map/second/pallas_call | solution.py:295
Async XLA Ops:
  2.5 14.9 %collective-permute-start = (f32[3,36,512]{2,1,0:T(8,128)S(1)}, f32[3,36,512]{2,1,0:T(8,128)S(1)}, u32[]{:S(2)}, u32[]{:S(2)}) collective-permute-start(f32[3,36,512]{2,1,0:T(8,128)S(1)} %get-tuple-element.22), channel_id=1, source_target_pairs={{0,1},{1,0},{2,3},{3,2},{4,5},{5,4},{6,7},{7,6},{8,9},{9,8},{10,11... | collective-permute-start | bytes 663560 | tf_op jit(solution)/shard_map/ppermute | solution.py:333
  4.0 13.4 %collective-permute-start.1 = (f32[3,36,512]{2,1,0:T(8,128)S(1)}, f32[3,36,512]{2,1,0:T(8,128)S(1)}, u32[]{:S(2)}, u32[]{:S(2)}) collective-permute-start(f32[3,36,512]{2,1,0:T(8,128)S(1)} %get-tuple-element.23), channel_id=1, source_target_pairs={{1,2},{2,1},{5,6},{6,5},{9,10},{10,9},{13,14},{14,13},{17,18},{18,... | collective-permute-start | bytes 663560 | tf_op jit(solution)/shard_map/ppermute | solution.py:334
  7.2 21.0 %all-to-all-start = ((f32[32,8,384]{2,1,0:T(8,128)}), f32[32,8,384]{2,1,0:T(8,128)S(1)}, u32[]{:S(2)}, u32[]{:S(2)}) async-start(f32[32,8,384]{2,1,0:T(8,128)} %bitcast.4), calls=%async_computation | async-start | bytes 786432 | tf_op jit(solution)/shard_map/all_to_all | solution.py:316
  31.5 15.5 %all-to-all-start.1 = ((f32[32,8,384]{2,1,0:T(8,128)}), f32[32,8,384]{2,1,0:T(8,128)S(1)}, u32[]{:S(2)}, u32[]{:S(2)}) async-start(f32[32,8,384]{2,1,0:T(8,128)} %bitcast.6), calls=%async_computation.1 | async-start | bytes 786432 | tf_op jit(solution)/shard_map/all_to_all | solution.py:316

commit v4 on v3

--- a/solution.py
+++ b/solution.py
@@ -42,6 +42,17 @@
     return jnp.concatenate([high, x - high], axis=0).astype(jnp.bfloat16)
 
 
+def pieces_with_coords(x):
+    top = []
+    for axis in range(2):
+        row = COORDS + 2 * axis
+        high = rounded(x[row : row + 1])
+        top += [high, x[row : row + 1] - high, x[row + 1 : row + 2]]
+    top.append(jnp.zeros((2, x.shape[1]), jnp.float32))
+    high = rounded(x)
+    return jnp.concatenate([jnp.concatenate(top, axis=0), high, x - high], axis=0).astype(jnp.bfloat16)
+
+
 def exact_rows(c):
     high = rounded(c)
     mid = rounded(c - high)
@@ -70,7 +81,8 @@
 
 def gather(pieces, entry_row, first):
     got = jnp.dot(pieces, one_hot(entry_row, first, pieces.shape[1]), preferred_element_type=jnp.float32)
-    return got[:ROWS] + got[ROWS:]
+    top = got.shape[0] - 2 * ROWS
+    return got[:top], got[top : top + ROWS] + got[top + ROWS :]
 
 
 def fill_coords(rows_ref, coords_ref):
@@ -98,8 +110,7 @@
     return jnp.where(lax.broadcasted_iota(jnp.int32, (GHOSTS, NP), 1) == node, 1.0, 0.0).astype(jnp.bfloat16)
 
 
-def pack(rows, send_ref, count_ref, packed_ref):
-    hot = packing_one_hot(send_ref[...], count_ref[...])
+def pack(hot, rows, packed_ref):
     high = rows.astype(jnp.bfloat16)
     low = (rows - high.astype(jnp.float32)).astype(jnp.bfloat16)
     dims = (((1,), (1,)), ((), ()))
@@ -125,9 +136,9 @@
     return [jnp.concatenate([jnp.concatenate(tiles, axis=0)] * (NP // 128), axis=1) for tiles in (cosine, sine)]
 
 
-def delta(got, coords, axis):
-    row = COORDS + 2 * axis
-    return (got[row : row + 1] + got[row + 1 : row + 2]) - coords[axis : axis + 1]
+def delta(place, coords, axis):
+    row = 3 * axis
+    return ((place[row : row + 1] + place[row + 1 : row + 2]) + place[row + 2 : row + 3]) - coords[axis : axis + 1]
 
 
 def facing(cosine, sine, delta_x, delta_y):
@@ -149,16 +160,16 @@
 def pack_kernel(
     band_ref, spectra_hbm, coords_hbm, send_hbm, count_hbm, wind_hbm, area_hbm, near_hbm,
     packed_ref, spectra_ref, coords_ref, send_ref, count_ref, wind_ref, area_ref, near_ref, near_edge_ref, far_edge_ref,
-    rows_ref, sems,
+    rows_ref, hot_ref, sems,
 ):
     odd = lax.rem(band_ref[0], 2)
     inner = pl.ds((1 - odd) * (BAND - DOWN_REACH), DOWN_REACH)
     outer = pl.ds(odd * (BAND - DOWN_REACH), DOWN_REACH)
     pairs = (
+        (send_hbm, send_ref),
+        (count_hbm, count_ref),
         (spectra_hbm, spectra_ref),
         (coords_hbm, coords_ref),
-        (send_hbm, send_ref),
-        (count_hbm, count_ref),
         (spectra_hbm.at[inner], near_edge_ref),
         (spectra_hbm.at[outer], far_edge_ref),
         (wind_hbm, wind_ref),
@@ -168,38 +179,43 @@
     copies = [pltpu.make_async_copy(source, target, sems.at[i]) for i, (source, target) in enumerate(pairs)]
     for copy in copies:
         copy.start()
-    for copy in copies[:4]:
+    for copy in copies[:2]:
+        copy.wait()
+    hot_ref[...] = packing_one_hot(send_ref[...], count_ref[...])
+    for copy in copies[2:4]:
         copy.wait()
     fill_rows(rows_ref, spectra_ref, coords_ref)
-    pack(rows_ref[...], send_ref, count_ref, packed_ref)
+    pack(hot_ref[...], rows_ref[...], packed_ref)
     for copy in copies[4:]:
         copy.wait()
 
 
-def local_kernel(
-    band_ref, spectra_ref, near_edge_ref, far_edge_ref, coords_ref, wind_ref, area_ref, near_ref,
-    base_ref, partial_ref, rows_ref,
-):
-    band = band_ref[0]
+def local_kernel(spectra_ref, coords_ref, area_ref, near_ref, partial_ref, rows_ref):
     coords = coords_ref[...]
     fill_rows(rows_ref, spectra_ref, coords_ref)
-    pieces = bf16_pieces(rows_ref[...])
+    pieces = pieces_with_coords(rows_ref[...])
     cosine, sine = directions()
     for k in range(K):
         entry = near_ref[k : k + 1, :]
-        got = gather(pieces, entry, 0)
-        delta_x = jnp.where(entry < NP, delta(got, coords, 0), 0.0)
-        delta_y = jnp.where(entry < NP, delta(got, coords, 1), 0.0)
+        place, got = gather(pieces, entry, 0)
+        delta_x = jnp.where(entry < NP, delta(place, coords, 0), 0.0)
+        delta_y = jnp.where(entry < NP, delta(place, coords, 1), 0.0)
         partial_ref[ROWS + k : ROWS + k + 1] = delta_x
         partial_ref[ROWS + K + k : ROWS + K + k + 1] = delta_y
         add_slot(partial_ref, partial_ref, facing(cosine, sine, delta_x, delta_y), got, k == 0)
     partial_ref[ROWS + 2 * K : ROWS + 2 * K + 1] = area_ref[...]
+
+
+def source_kernel(band_ref, spectra_ref, near_edge_ref, far_edge_ref, wind_ref, base_ref):
+    band = band_ref[0]
+    cosine, sine = directions()
     along = cosine[:ND] * wind_ref[0:1, :] + sine[:ND] * wind_ref[1:2, :]
     odd = lax.rem(band, 2) == 1
     lower = [jnp.where(odd, near_edge_ref[f], far_edge_ref[f]) for f in range(DOWN_REACH)]
     upper = [jnp.where(odd, far_edge_ref[f], near_edge_ref[f]) for f in range(UP_REACH)]
     base_ref[COORDS:] = jnp.zeros((ROWS - COORDS, NP), jnp.float32)
-    for f in range(BAND):
+
+    def source(f):
         density = spectra_ref[f]
         up = spectra_ref[f + UP_REACH] if f + UP_REACH < BAND else upper[f + UP_REACH - BAND]
         down = spectra_ref[f - DOWN_REACH] if f >= DOWN_REACH else lower[f]
@@ -212,6 +228,9 @@
         growth = wind_growth * jnp.maximum(ratio_of(band, f) * along - 1.0, 0.0)
         base_ref[f * ND : (f + 1) * ND] = density + time_step * (quad + growth * density)
 
+    for f in range(BAND):
+        source(f)
+
 
 def settle(band, base_ref, area, total_ref, weight, group, target_ref):
     start, size = group
@@ -222,8 +241,8 @@
     target_ref[rows] = (base_ref[rows] + scaled * total_ref[rows]) / (1.0 + scaled * weight[:size])
 
 
-def ghost_pieces(ghost_ref):
-    return bf16_pieces(ghost_ref[...].T[:ROWS])
+def ghost_rows(ghost_ref):
+    return ghost_ref[...].T[:ROWS]
 
 
 def first_kernel(
@@ -232,14 +251,14 @@
 ):
     band = band_ref[0]
     coords = coords_ref[...]
-    pieces = ghost_pieces(ghost_ref)
+    pieces = pieces_with_coords(ghost_rows(ghost_ref))
     cosine, sine = directions()
     weight = jnp.zeros((PAIR, NP), jnp.float32)
     for k in range(K):
         entry = near_ref[k : k + 1, :]
-        got = gather(pieces, entry, NP)
-        delta_x = jnp.where(entry < NP, partial_ref[ROWS + k : ROWS + k + 1], delta(got, coords, 0))
-        delta_y = jnp.where(entry < NP, partial_ref[ROWS + K + k : ROWS + K + k + 1], delta(got, coords, 1))
+        place, got = gather(pieces, entry, NP)
+        delta_x = jnp.where(entry < NP, partial_ref[ROWS + k : ROWS + k + 1], delta(place, coords, 0))
+        delta_y = jnp.where(entry < NP, partial_ref[ROWS + K + k : ROWS + K + k + 1], delta(place, coords, 1))
         delta_ref[k : k + 1, :] = delta_x
         delta_ref[K + k : K + k + 1, :] = delta_y
         inflow = facing(cosine, sine, delta_x, delta_y)
@@ -249,14 +268,14 @@
     delta_ref[2 * K : 2 * K + 1, :] = area
     for group in GROUPS:
         settle(band, base_ref, area, total_ref, weight, group, total_ref)
-    pack(total_ref[...], send_ref, count_ref, packed_ref)
+    pack(packing_one_hot(send_ref[...], count_ref[...]), total_ref[...], packed_ref)
 
 
 def second_local_kernel(current_ref, delta_ref, near_ref, partial_ref):
     pieces = bf16_pieces(current_ref[...])
     cosine, sine = directions()
     for k in range(K):
-        got = gather(pieces, near_ref[k : k + 1, :], 0)
+        _, got = gather(pieces, near_ref[k : k + 1, :], 0)
         inflow = facing(cosine, sine, delta_ref[k : k + 1, :], delta_ref[K + k : K + k + 1, :])
         add_slot(partial_ref, partial_ref, inflow, got, k == 0)
 
@@ -265,11 +284,11 @@
     band_ref, ghost_ref, base_ref, partial_ref, delta_ref, near_ref, out_ref, total_ref, planes_ref, sems
 ):
     band = band_ref[0]
-    pieces = ghost_pieces(ghost_ref)
+    pieces = bf16_pieces(ghost_rows(ghost_ref))
     cosine, sine = directions()
     weight = jnp.zeros((PAIR, NP), jnp.float32)
     for k in range(K):
-        got = gather(pieces, near_ref[k : k + 1, :], NP)
+        _, got = gather(pieces, near_ref[k : k + 1, :], NP)
         inflow = facing(cosine, sine, delta_ref[k : k + 1, :], delta_ref[K + k : K + k + 1, :])
         weight = weight + inflow
         add_slot(total_ref, partial_ref if k == 0 else total_ref, inflow, got, False)
@@ -300,7 +319,6 @@
         scratch_shapes=scratch,
         compiler_params=pltpu.CompilerParams(vmem_limit_bytes=24 << 20),
         name=name,
-        cost_estimate=pl.CostEstimate(flops=10**10, transcendentals=0, bytes_accessed=10**10),
     )(*[pltpu.with_memory_space_constraint(array, HBM) if memory is HBM else array for array, memory in operands])
 
 
@@ -324,7 +342,7 @@
         [((GHOSTS, LANES), f32, VMEM)]
         + [(array.shape, array.dtype, VMEM) for array in inputs]
         + [((DOWN_REACH, ND, NP), f32, VMEM)] * 2,
-        [rows, dma((len(inputs) + 2,))],
+        [rows, pltpu.VMEM((GHOSTS, NP), jnp.bfloat16), dma((len(inputs) + 2,))],
         "pack",
         (band, SMEM),
         *[(array, HBM) for array in inputs],
@@ -333,13 +351,20 @@
     near_edge = lax.ppermute(near_edge, "freq", pairs[0])
     far_edge = lax.ppermute(far_edge, "freq", pairs[1])
     ghosts = exchange(packed)
-    base, partial = call(
+    (partial,) = call(
         local_kernel,
-        [((ROWS, NP), f32, VMEM), ((ROWS + 3 * K, NP), f32, VMEM)],
+        [((ROWS + 3 * K, NP), f32, VMEM)],
         [rows],
         "local_first",
+        *inside(spectra, coords, area, near),
+    )
+    (base,) = call(
+        source_kernel,
+        [((ROWS, NP), f32, VMEM)],
+        [],
+        "source",
         (band, SMEM),
-        *inside(spectra, near_edge, far_edge, coords, wind, area, near),
+        *inside(spectra, near_edge, far_edge, wind),
     )
     packed, current, deltas = call(
         first_kernel,

time: 50 us -> 49.5 us (0.990)
  starting transfers between devices: 19 us -> 22.9 us
  waiting for transfers between devices: 14.4 us -> 10.9 us
  Pallas kernels: 16 us -> 15.1 us
    all_to_all x2, waiting for transfers between devices: 14.4 us -> 7.15 us  [exchange(): lax.all_to_all(packed, 'mesh', split_axis=0, concat_axis=0, tiled=True)]
    all_to_all x2, starting transfers between devices: 14.3 us -> 19.7 us  [exchange(): lax.all_to_all(packed, 'mesh', split_axis=0, concat_axis=0, tiled=True)]
    ppermute x1, waiting for transfers between devices: 0.01 us -> 3.7 us  [local(): far_edge = lax.ppermute(far_edge, 'freq', pairs[1])]
    ppermute x1, starting transfers between devices: 3.19 us -> 2.2 us  [local(): far_edge = lax.ppermute(far_edge, 'freq', pairs[1])]
    pallas_call x5 -> x6, Pallas kernels: 16 us -> 15.1 us  [call(): pl.pallas_call(kernel, out_shape=[jax.ShapeDtypeStruct(shape, dtype) for...]
  transfers between devices with their start and end apart: 4 -> 4, of which waited for: 2 -> 2; matrix products, arithmetic and copies ran while one was open for 0% -> 0% of each run, Pallas kernels for 16% -> 14%
where the time goes in v4:
time: 49.5 us; the launch traced here: 49.2 us
  starting transfers between devices  22.9 us (46%)
  Pallas kernels  15.1 us (31%)
  waiting for transfers between devices  10.9 us (22%)
    all_to_all x2, starting transfers between devices, exchange(): lax.all_to_all(packed, 'mesh', split_axis=0, concat_axis=0, tiled=True)  19.7 us
    pallas_call x6, Pallas kernels, call(): pl.pallas_call(kernel, out_shape=[jax.ShapeDtypeStruct(shape, dtype) for...  15.1 us
    all_to_all x2, waiting for transfers between devices, exchange(): lax.all_to_all(packed, 'mesh', split_axis=0, concat_axis=0, tiled=True)  7.15 us
    ppermute x1, waiting for transfers between devices, local(): far_edge = lax.ppermute(far_edge, 'freq', pairs[1])  3.7 us
    ppermute x1, starting transfers between devices, local(): far_edge = lax.ppermute(far_edge, 'freq', pairs[1])  2.2 us
    ppermute x1, starting transfers between devices, local(): near_edge = lax.ppermute(near_edge, 'freq', pairs[0])  1.04 us
  transfers between devices with their start and end apart: 4, of which 2 were waited for; matrix products, arithmetic and copies ran while one was open for 0% of the time, Pallas kernels for 14%

profile of v4, /device:TPU:1, one launch (start us, length us, event | category | flops | bytes accessed | tf_op | source)
XLA Modules:
  0.0 49.2 jit_solution(961517656720190083)
XLA Ops:
  0.0 2.5 %pack.1 = (f32[256,384]{1,0:T(8,128)}, f32[9,36,512]{2,1,0:T(8,128)S(1)}, f32[2,512]{1,0:T(2,128)S(1)}, s32[8,32]{1,0:T(8,128)S(1)}, s32[1,32]{1,0:T(1,128)S(1)}...) custom-call(s32[1]{0:T(128)} %bitcast.band_ref, ...), custom_call_target="tpu_custom_call" | custom-call | tf_op jit(solution)/shard_map/pack/pallas_call | solution.py:314
  2.5 11.4 %all-to-all-start = ((f32[32,8,384]{2,1,0:T(8,128)}), f32[32,8,384]{2,1,0:T(8,128)S(1)}, u32[]{:S(2)}, u32[]{:S(2)}) async-start(f32[32,8,384]{2,1,0:T(8,128)} %bitcast.4), calls=%async_computation | async-start | bytes 786432 | tf_op jit(solution)/shard_map/all_to_all | solution.py:334
  13.8 1.0 %collective-permute-start = (f32[3,36,512]{2,1,0:T(8,128)S(1)}, f32[3,36,512]{2,1,0:T(8,128)S(1)}, u32[]{:S(2)}, u32[]{:S(2)}) collective-permute-start(f32[3,36,512]{2,1,0:T(8,128)S(1)} %get-tuple-element.20), channel_id=1, source_target_pairs={{0,1},{1,0},{2,3},{3,2},{4,5},{5,4},{6,7},{7,6},{8,9},{9,8},{10,11... | collective-permute-start | bytes 663560 | tf_op jit(solution)/shard_map/ppermute | solution.py:351
  14.9 2.2 %collective-permute-start.1 = (f32[3,36,512]{2,1,0:T(8,128)S(1)}, f32[3,36,512]{2,1,0:T(8,128)S(1)}, u32[]{:S(2)}, u32[]{:S(2)}) collective-permute-start(f32[3,36,512]{2,1,0:T(8,128)S(1)} %get-tuple-element.21), channel_id=1, source_target_pairs={{1,2},{2,1},{5,6},{6,5},{9,10},{10,9},{13,14},{14,13},{17,18},{18,... | collective-permute-start | bytes 663560 | tf_op jit(solution)/shard_map/ppermute | solution.py:352
  17.1 3.1 %local_first.1.partial_ref = f32[352,512]{1,0:T(8,128)S(1)} custom-call(f32[9,36,512]{2,1,0:T(8,128)S(1)} %get-tuple-element.19.spectra_ref, f32[2,512]{1,0:T(2,128)S(1)} %get-tuple-element.23.coords_ref, f32[1,512]{1,0:T(1,128)S(1)} %get-tuple-element.24.area_ref, s32[8,512]{1,0:T(8,128)S(1)} %get-tuple-element.25.near_ref), custom_call_target="tpu_custom_call" | custom-call | tf_op jit(solution)/shard_map/local_first/pallas_call | solution.py:314
  20.2 0.0 collective-permute-done.near_edge_ref
  20.2 3.7 %collective-permute-done.1.far_edge_ref = f32[3,36,512]{2,1,0:T(8,128)S(1)} collective-permute-done((f32[3,36,512]{2,1,0:T(8,128)S(1)}, f32[3,36,512]{2,1,0:T(8,128)S(1)}, u32[]{:S(2)}, u32[]{:S(2)}) %collective-permute-start.1) | collective-permute-done | bytes 221216 | tf_op jit(solution)/shard_map/ppermute | solution.py:352
  23.9 0.8 %source.1.base_ref = f32[328,512]{1,0:T(8,128)S(1)} custom-call(s32[1]{0:T(128)} %bitcast.band_ref, f32[9,36,512]{2,1,0:T(8,128)S(1)} %get-tuple-element.19.spectra_ref, f32[3,36,512]{2,1,0:T(8,128)S(1)} %collective-permute-done.near_edge_ref, f32[3,36,512]{2,1,0:T(8,128)S(1)} %collective-permute-done.1.far_edge_ref, f32[2,512]{1,0:T(2,128)S(1)} %get-tuple-element.22.wind_ref), custom_call_target="tpu_custom_call" | custom-call | tf_op jit(solution)/shard_map/source/pallas_call | solution.py:314
  24.7 0.0 all-to-all-done
  24.7 3.1 %first.1 = (f32[256,384]{1,0:T(8,128)}, f32[328,512]{1,0:T(8,128)S(1)}, f32[24,512]{1,0:T(8,128)S(1)}) custom-call(s32[1]{0:T(128)} %bitcast.band_ref, f32[256,384]{1,0:T(8,128)S(1)} %bitcast.8, f32[328,512]{1,0:T(8,128)S(1)} %source.1.base_ref, f32[352,512]{1,0:T(8,128)S(1)} %local_first.1.partial_ref, f32[2,512]{1,0:T(2,128)S(1)} %get-tuple-element.23.coords_ref, ...), custom_call_target="tpu_custom_call" | custom-call | tf_op jit(solution)/shard_map/first/pallas_call | solution.py:314
  27.8 8.4 %all-to-all-start.1 = ((f32[32,8,384]{2,1,0:T(8,128)}), f32[32,8,384]{2,1,0:T(8,128)S(1)}, u32[]{:S(2)}, u32[]{:S(2)}) async-start(f32[32,8,384]{2,1,0:T(8,128)} %bitcast.6), calls=%async_computation.1 | async-start | bytes 786432 | tf_op jit(solution)/shard_map/all_to_all | solution.py:334
  36.2 3.1 %local_second.1.partial_ref = f32[328,512]{1,0:T(8,128)S(1)} custom-call(f32[328,512]{1,0:T(8,128)S(1)} %get-tuple-element.29.current_ref, f32[24,512]{1,0:T(8,128)S(1)} %get-tuple-element.30.delta_ref, s32[8,512]{1,0:T(8,128)S(1)} %get-tuple-element.25.near_ref), custom_call_target="tpu_custom_call" | custom-call | tf_op jit(solution)/shard_map/local_second/pallas_call | solution.py:314
  39.3 7.1 %all-to-all-done.1 = f32[32,8,384]{2,1,0:T(8,128)S(1)} async-done(((f32[32,8,384]{2,1,0:T(8,128)}), f32[32,8,384]{2,1,0:T(8,128)S(1)}, u32[]{:S(2)}, u32[]{:S(2)}) %all-to-all-start.1) | async-done | bytes 393248 | tf_op jit(solution)/shard_map/all_to_all | solution.py:334
  46.5 2.5 %second.1 = f32[9,36,512]{2,1,0:T(8,128)} custom-call(s32[1]{0:T(128)} %bitcast.band_ref, f32[256,384]{1,0:T(8,128)S(1)} %bitcast.9, f32[328,512]{1,0:T(8,128)S(1)} %source.1.base_ref, f32[328,512]{1,0:T(8,128)S(1)} %local_second.1.partial_ref, f32[24,512]{1,0:T(8,128)S(1)} %get-tuple-element.30.delta_ref, s32[8,512]{1,0:T(8,128)S(1)} %get-tuple-element.25.near_ref), custom_call_target="tpu_custom_call" | custom-call | tf_op jit(solution)/shard_map/second/pallas_call | solution.py:314
Async XLA Ops:
  2.5 22.3 %all-to-all-start = ((f32[32,8,384]{2,1,0:T(8,128)}), f32[32,8,384]{2,1,0:T(8,128)S(1)}, u32[]{:S(2)}, u32[]{:S(2)}) async-start(f32[32,8,384]{2,1,0:T(8,128)} %bitcast.4), calls=%async_computation | async-start | bytes 786432 | tf_op jit(solution)/shard_map/all_to_all | solution.py:334
  13.8 6.4 %collective-permute-start = (f32[3,36,512]{2,1,0:T(8,128)S(1)}, f32[3,36,512]{2,1,0:T(8,128)S(1)}, u32[]{:S(2)}, u32[]{:S(2)}) collective-permute-start(f32[3,36,512]{2,1,0:T(8,128)S(1)} %get-tuple-element.20), channel_id=1, source_target_pairs={{0,1},{1,0},{2,3},{3,2},{4,5},{5,4},{6,7},{7,6},{8,9},{9,8},{10,11... | collective-permute-start | bytes 663560 | tf_op jit(solution)/shard_map/ppermute | solution.py:351
  14.9 9.0 %collective-permute-start.1 = (f32[3,36,512]{2,1,0:T(8,128)S(1)}, f32[3,36,512]{2,1,0:T(8,128)S(1)}, u32[]{:S(2)}, u32[]{:S(2)}) collective-permute-start(f32[3,36,512]{2,1,0:T(8,128)S(1)} %get-tuple-element.21), channel_id=1, source_target_pairs={{1,2},{2,1},{5,6},{6,5},{9,10},{10,9},{13,14},{14,13},{17,18},{18,... | collective-permute-start | bytes 663560 | tf_op jit(solution)/shard_map/ppermute | solution.py:352
  27.8 18.6 %all-to-all-start.1 = ((f32[32,8,384]{2,1,0:T(8,128)}), f32[32,8,384]{2,1,0:T(8,128)S(1)}, u32[]{:S(2)}, u32[]{:S(2)}) async-start(f32[32,8,384]{2,1,0:T(8,128)} %bitcast.6), calls=%async_computation.1 | async-start | bytes 786432 | tf_op jit(solution)/shard_map/all_to_all | solution.py:334

commit v5 on v4

--- a/solution.py
+++ b/solution.py
@@ -190,11 +190,44 @@
         copy.wait()
 
 
-def local_kernel(spectra_ref, coords_ref, area_ref, near_ref, partial_ref, rows_ref):
+def source(f, band, spectra_ref, lower_ref, upper_ref, along, base_ref):
+    density = spectra_ref[f]
+    up = spectra_ref[f + UP_REACH] if f + UP_REACH < BAND else upper_ref[f + UP_REACH - BAND]
+    down = spectra_ref[f - DOWN_REACH] if f >= DOWN_REACH else lower_ref[f]
+    up_left, up_right = rolled(up, -UP_SHIFT), rolled(up, UP_SHIFT)
+    down_left, down_right = rolled(down, DOWN_SHIFT), rolled(down, -DOWN_SHIFT)
+    quad = quad_coupling * (
+        density * density * (up_left + down_left + up_right + down_right)
+        - 2.0 * density * (up_left * down_left + up_right * down_right)
+    )
+    growth = wind_growth * jnp.maximum(ratio_of(band, f) * along - 1.0, 0.0)
+    base_ref[f * ND : (f + 1) * ND] = density + time_step * (quad + growth * density)
+
+
+def edge_sources(is_lower, edge_ref, band, spectra_ref, along, base_ref):
+    @pl.when(is_lower)
+    def _():
+        for f in range(DOWN_REACH):
+            source(f, band, spectra_ref, edge_ref, None, along, base_ref)
+
+    @pl.when(jnp.logical_not(is_lower))
+    def _():
+        for f in range(BAND - UP_REACH, BAND):
+            source(f, band, spectra_ref, None, edge_ref, along, base_ref)
+
+
+def local_kernel(
+    band_ref, spectra_ref, near_edge_ref, coords_ref, wind_ref, area_ref, near_ref, base_ref, partial_ref, rows_ref
+):
+    band = band_ref[0]
     coords = coords_ref[...]
     fill_rows(rows_ref, spectra_ref, coords_ref)
     pieces = pieces_with_coords(rows_ref[...])
     cosine, sine = directions()
+    along = cosine[:ND] * wind_ref[0:1, :] + sine[:ND] * wind_ref[1:2, :]
+    base_ref[COORDS:] = jnp.zeros((ROWS - COORDS, NP), jnp.float32)
+    for f in range(DOWN_REACH, BAND - UP_REACH):
+        source(f, band, spectra_ref, None, None, along, base_ref)
     for k in range(K):
         entry = near_ref[k : k + 1, :]
         place, got = gather(pieces, entry, 0)
@@ -204,32 +237,7 @@
         partial_ref[ROWS + K + k : ROWS + K + k + 1] = delta_y
         add_slot(partial_ref, partial_ref, facing(cosine, sine, delta_x, delta_y), got, k == 0)
     partial_ref[ROWS + 2 * K : ROWS + 2 * K + 1] = area_ref[...]
-
-
-def source_kernel(band_ref, spectra_ref, near_edge_ref, far_edge_ref, wind_ref, base_ref):
-    band = band_ref[0]
-    cosine, sine = directions()
-    along = cosine[:ND] * wind_ref[0:1, :] + sine[:ND] * wind_ref[1:2, :]
-    odd = lax.rem(band, 2) == 1
-    lower = [jnp.where(odd, near_edge_ref[f], far_edge_ref[f]) for f in range(DOWN_REACH)]
-    upper = [jnp.where(odd, far_edge_ref[f], near_edge_ref[f]) for f in range(UP_REACH)]
-    base_ref[COORDS:] = jnp.zeros((ROWS - COORDS, NP), jnp.float32)
-
-    def source(f):
-        density = spectra_ref[f]
-        up = spectra_ref[f + UP_REACH] if f + UP_REACH < BAND else upper[f + UP_REACH - BAND]
-        down = spectra_ref[f - DOWN_REACH] if f >= DOWN_REACH else lower[f]
-        up_left, up_right = rolled(up, -UP_SHIFT), rolled(up, UP_SHIFT)
-        down_left, down_right = rolled(down, DOWN_SHIFT), rolled(down, -DOWN_SHIFT)
-        quad = quad_coupling * (
-            density * density * (up_left + down_left + up_right + down_right)
-            - 2.0 * density * (up_left * down_left + up_right * down_right)
-        )
-        growth = wind_growth * jnp.maximum(ratio_of(band, f) * along - 1.0, 0.0)
-        base_ref[f * ND : (f + 1) * ND] = density + time_step * (quad + growth * density)
-
-    for f in range(BAND):
-        source(f)
+    edge_sources(lax.rem(band, 2) == 1, near_edge_ref, band, spectra_ref, along, base_ref)
 
 
 def settle(band, base_ref, area, total_ref, weight, group, target_ref):
@@ -245,11 +253,7 @@
     return ghost_ref[...].T[:ROWS]
 
 
-def first_kernel(
-    band_ref, ghost_ref, base_ref, partial_ref, coords_ref, near_ref, send_ref, count_ref,
-    packed_ref, total_ref, delta_ref,
-):
-    band = band_ref[0]
+def first_gather_kernel(ghost_ref, partial_ref, coords_ref, near_ref, total_ref, weight_ref, delta_ref):
     coords = coords_ref[...]
     pieces = pieces_with_coords(ghost_rows(ghost_ref))
     cosine, sine = directions()
@@ -264,11 +268,23 @@
         inflow = facing(cosine, sine, delta_x, delta_y)
         weight = weight + inflow
         add_slot(total_ref, partial_ref if k == 0 else total_ref, inflow, got, False)
-    area = partial_ref[ROWS + 2 * K : ROWS + 2 * K + 1]
-    delta_ref[2 * K : 2 * K + 1, :] = area
+    weight_ref[...] = weight
+    delta_ref[2 * K : 2 * K + 1, :] = partial_ref[ROWS + 2 * K : ROWS + 2 * K + 1]
+
+
+def first_settle_kernel(
+    band_ref, spectra_ref, far_edge_ref, wind_ref, part_ref, total_ref, weight_ref, delta_ref, send_ref, count_ref,
+    packed_ref, current_ref, base_ref,
+):
+    band = band_ref[0]
+    cosine, sine = directions()
+    along = cosine[:ND] * wind_ref[0:1, :] + sine[:ND] * wind_ref[1:2, :]
+    base_ref[...] = part_ref[...]
+    edge_sources(lax.rem(band, 2) == 0, far_edge_ref, band, spectra_ref, along, base_ref)
+    area, weight = delta_ref[2 * K : 2 * K + 1], weight_ref[...]
     for group in GROUPS:
-        settle(band, base_ref, area, total_ref, weight, group, total_ref)
-    pack(packing_one_hot(send_ref[...], count_ref[...]), total_ref[...], packed_ref)
+        settle(band, base_ref, area, total_ref, weight, group, current_ref)
+    pack(packing_one_hot(send_ref[...], count_ref[...]), current_ref[...], packed_ref)
 
 
 def second_local_kernel(current_ref, delta_ref, near_ref, partial_ref):
@@ -351,28 +367,28 @@
     near_edge = lax.ppermute(near_edge, "freq", pairs[0])
     far_edge = lax.ppermute(far_edge, "freq", pairs[1])
     ghosts = exchange(packed)
-    (partial,) = call(
+    base, partial = call(
         local_kernel,
-        [((ROWS + 3 * K, NP), f32, VMEM)],
+        [((ROWS, NP), f32, VMEM), ((ROWS + 3 * K, NP), f32, VMEM)],
         [rows],
         "local_first",
-        *inside(spectra, coords, area, near),
-    )
-    (base,) = call(
-        source_kernel,
-        [((ROWS, NP), f32, VMEM)],
+        (band, SMEM),
+        *inside(spectra, near_edge, coords, wind, area, near),
+    )
+    total, weight, deltas = call(
+        first_gather_kernel,
+        [((ROWS, NP), f32, VMEM), ((PAIR, NP), f32, VMEM), ((3 * K, NP), f32, VMEM)],
         [],
-        "source",
+        "first_gather",
+        *inside(ghosts, partial, coords, near),
+    )
+    packed, current, base = call(
+        first_settle_kernel,
+        [((GHOSTS, LANES), f32, VMEM), ((ROWS, NP), f32, VMEM), ((ROWS, NP), f32, VMEM)],
+        [],
+        "first_settle",
         (band, SMEM),
-        *inside(spectra, near_edge, far_edge, wind),
-    )
-    packed, current, deltas = call(
-        first_kernel,
-        [((GHOSTS, LANES), f32, VMEM), ((ROWS, NP), f32, VMEM), ((3 * K, NP), f32, VMEM)],
-        [],
-        "first",
-        (band, SMEM),
-        *inside(ghosts, base, partial, coords, near, send, count),
+        *inside(spectra, far_edge, wind, base, total, weight, deltas, send, count),
     )
     ghosts = exchange(packed)
     (partial,) = call(

time: 49.5 us -> 48.8 us (0.986)
  starting transfers between devices: 22.9 us -> 21.8 us
    all_to_all x2, waiting for transfers between devices: 7.15 us -> 11.2 us  [exchange(): lax.all_to_all(packed, 'mesh', split_axis=0, concat_axis=0, tiled=True)]
    ppermute x1, waiting for transfers between devices: 3.7 us -> 0.01 us  [local(): far_edge = lax.ppermute(far_edge, 'freq', pairs[1])]
    all_to_all x2, starting transfers between devices: 19.7 us -> 18.6 us  [exchange(): lax.all_to_all(packed, 'mesh', split_axis=0, concat_axis=0, tiled=True)]
  transfers between devices with their start and end apart: 4 -> 4, of which waited for: 2 -> 2; matrix products, arithmetic and copies ran while one was open for 0% -> 0% of each run, Pallas kernels for 14% -> 18%
where the time goes in v5:
time: 48.8 us; the launch traced here: 48.4 us
  starting transfers between devices  21.8 us (45%)
  Pallas kernels  15.2 us (31%)
  waiting for transfers between devices  11.2 us (23%)
    all_to_all x2, starting transfers between devices, exchange(): lax.all_to_all(packed, 'mesh', split_axis=0, concat_axis=0, tiled=True)  18.6 us
    pallas_call x6, Pallas kernels, call(): pl.pallas_call(kernel, out_shape=[jax.ShapeDtypeStruct(shape, dtype) for...  15.2 us
    all_to_all x2, waiting for transfers between devices, exchange(): lax.all_to_all(packed, 'mesh', split_axis=0, concat_axis=0, tiled=True)  11.2 us
    ppermute x1, starting transfers between devices, local(): far_edge = lax.ppermute(far_edge, 'freq', pairs[1])  2.2 us
    ppermute x1, starting transfers between devices, local(): near_edge = lax.ppermute(near_edge, 'freq', pairs[0])  1.04 us
  transfers between devices with their start and end apart: 4, of which 2 were waited for; matrix products, arithmetic and copies ran while one was open for 0% of the time, Pallas kernels for 18%

profile of v5, /device:TPU:1, one launch (start us, length us, event | category | flops | bytes accessed | tf_op | source)
XLA Modules:
  0.0 48.4 jit_solution(7431242947043619889)
XLA Ops:
  0.0 2.5 %pack.1 = (f32[256,384]{1,0:T(8,128)}, f32[9,36,512]{2,1,0:T(8,128)S(1)}, f32[2,512]{1,0:T(2,128)S(1)}, s32[8,32]{1,0:T(8,128)S(1)}, s32[1,32]{1,0:T(1,128)S(1)}...) custom-call(s32[1]{0:T(128)} %bitcast.band_ref, ...), custom_call_target="tpu_custom_call" | custom-call | tf_op jit(solution)/shard_map/pack/pallas_call | solution.py:330
  2.5 11.4 %all-to-all-start = ((f32[32,8,384]{2,1,0:T(8,128)}), f32[32,8,384]{2,1,0:T(8,128)S(1)}, u32[]{:S(2)}, u32[]{:S(2)}) async-start(f32[32,8,384]{2,1,0:T(8,128)} %bitcast.4), calls=%async_computation | async-start | bytes 786432 | tf_op jit(solution)/shard_map/all_to_all | solution.py:350
  13.8 1.0 %collective-permute-start.1 = (f32[3,36,512]{2,1,0:T(8,128)S(1)}, f32[3,36,512]{2,1,0:T(8,128)S(1)}, u32[]{:S(2)}, u32[]{:S(2)}) collective-permute-start(f32[3,36,512]{2,1,0:T(8,128)S(1)} %get-tuple-element.26), channel_id=1, source_target_pairs={{0,1},{1,0},{2,3},{3,2},{4,5},{5,4},{6,7},{7,6},{8,9},{9,8},{10,11... | collective-permute-start | bytes 663560 | tf_op jit(solution)/shard_map/ppermute | solution.py:367
  14.9 2.2 %collective-permute-start = (f32[3,36,512]{2,1,0:T(8,128)S(1)}, f32[3,36,512]{2,1,0:T(8,128)S(1)}, u32[]{:S(2)}, u32[]{:S(2)}) collective-permute-start(f32[3,36,512]{2,1,0:T(8,128)S(1)} %get-tuple-element.24), channel_id=1, source_target_pairs={{1,2},{2,1},{5,6},{6,5},{9,10},{10,9},{13,14},{14,13},{17,18},{18,... | collective-permute-start | bytes 663560 | tf_op jit(solution)/shard_map/ppermute | solution.py:368
  17.1 0.0 collective-permute-done.1.near_edge_ref
  17.1 3.8 %local_first.1 = (f32[328,512]{1,0:T(8,128)S(1)}, f32[352,512]{1,0:T(8,128)S(1)}) custom-call(s32[1]{0:T(128)} %bitcast.band_ref, f32[9,36,512]{2,1,0:T(8,128)S(1)} %get-tuple-element.23.spectra_ref, f32[3,36,512]{2,1,0:T(8,128)S(1)} %collective-permute-done.1.near_edge_ref, f32[2,512]{1,0:T(2,128)S(1)} %get-tuple-element.27.coords_ref, ...), custom_call_target="tpu_custom_call" | custom-call | tf_op jit(solution)/shard_map/local_first/pallas_call | solution.py:330
  20.9 3.1 %all-to-all-done = f32[32,8,384]{2,1,0:T(8,128)S(1)} async-done(((f32[32,8,384]{2,1,0:T(8,128)}), f32[32,8,384]{2,1,0:T(8,128)S(1)}, u32[]{:S(2)}, u32[]{:S(2)}) %all-to-all-start) | async-done | bytes 393248 | tf_op jit(solution)/shard_map/all_to_all | solution.py:350
  24.0 1.8 %first_gather.1 = (f32[328,512]{1,0:T(8,128)S(1)}, f32[72,512]{1,0:T(8,128)S(1)}, f32[24,512]{1,0:T(8,128)S(1)}) custom-call(f32[256,384]{1,0:T(8,128)S(1)} %bitcast.8, f32[352,512]{1,0:T(8,128)S(1)} %get-tuple-element.32.partial_ref, f32[2,512]{1,0:T(2,128)S(1)} %get-tuple-element.27.coords_ref, s32[8,512]{1,0:T(8,128)S(1)} %get-tuple-element.29.near_ref), custom_call_target="tpu_custom_call" | custom-call | tf_op jit(solution)/shard_map/first_gather/pallas_call | solution.py:330
  25.7 0.0 collective-permute-done.far_edge_ref
  25.8 1.6 %first_settle.1 = (f32[256,384]{1,0:T(8,128)}, f32[328,512]{1,0:T(8,128)S(1)}, f32[328,512]{1,0:T(8,128)S(1)}) custom-call(s32[1]{0:T(128)} %bitcast.band_ref, f32[9,36,512]{2,1,0:T(8,128)S(1)} %get-tuple-element.23.spectra_ref, f32[3,36,512]{2,1,0:T(8,128)S(1)} %collective-permute-done.far_edge_ref, f32[2,512]{1,0:T(2,128)S(1)} %get-tuple-element.25.wind_ref, ...), custom_call_target="tpu_custom_call" | custom-call | tf_op jit(solution)/shard_map/first_settle/pallas_call | solution.py:330
  27.4 7.2 %all-to-all-start.1 = ((f32[32,8,384]{2,1,0:T(8,128)}), f32[32,8,384]{2,1,0:T(8,128)S(1)}, u32[]{:S(2)}, u32[]{:S(2)}) async-start(f32[32,8,384]{2,1,0:T(8,128)} %bitcast.6), calls=%async_computation.1 | async-start | bytes 786432 | tf_op jit(solution)/shard_map/all_to_all | solution.py:350
  34.6 3.1 %local_second.1.partial_ref = f32[328,512]{1,0:T(8,128)S(1)} custom-call(f32[328,512]{1,0:T(8,128)S(1)} %get-tuple-element.40.current_ref, f32[24,512]{1,0:T(8,128)S(1)} %get-tuple-element.35.delta_ref, s32[8,512]{1,0:T(8,128)S(1)} %get-tuple-element.29.near_ref), custom_call_target="tpu_custom_call" | custom-call | tf_op jit(solution)/shard_map/local_second/pallas_call | solution.py:330
  37.7 8.1 %all-to-all-done.1 = f32[32,8,384]{2,1,0:T(8,128)S(1)} async-done(((f32[32,8,384]{2,1,0:T(8,128)}), f32[32,8,384]{2,1,0:T(8,128)S(1)}, u32[]{:S(2)}, u32[]{:S(2)}) %all-to-all-start.1) | async-done | bytes 393248 | tf_op jit(solution)/shard_map/all_to_all | solution.py:350
  45.7 2.5 %second.1 = f32[9,36,512]{2,1,0:T(8,128)} custom-call(s32[1]{0:T(128)} %bitcast.band_ref, f32[256,384]{1,0:T(8,128)S(1)} %bitcast.9, f32[328,512]{1,0:T(8,128)S(1)} %get-tuple-element.39.base_ref, f32[328,512]{1,0:T(8,128)S(1)} %local_second.1.partial_ref, f32[24,512]{1,0:T(8,128)S(1)} %get-tuple-element.35.delta_ref, s32[8,512]{1,0:T(8,128)S(1)} %get-tuple-element.29.near_ref), custom_call_target="tpu_custom_call" | custom-call | tf_op jit(solution)/shard_map/second/pallas_call | solution.py:330
Async XLA Ops:
  2.5 21.5 %all-to-all-start = ((f32[32,8,384]{2,1,0:T(8,128)}), f32[32,8,384]{2,1,0:T(8,128)S(1)}, u32[]{:S(2)}, u32[]{:S(2)}) async-start(f32[32,8,384]{2,1,0:T(8,128)} %bitcast.4), calls=%async_computation | async-start | bytes 786432 | tf_op jit(solution)/shard_map/all_to_all | solution.py:350
  13.8 3.3 %collective-permute-start.1 = (f32[3,36,512]{2,1,0:T(8,128)S(1)}, f32[3,36,512]{2,1,0:T(8,128)S(1)}, u32[]{:S(2)}, u32[]{:S(2)}) collective-permute-start(f32[3,36,512]{2,1,0:T(8,128)S(1)} %get-tuple-element.26), channel_id=1, source_target_pairs={{0,1},{1,0},{2,3},{3,2},{4,5},{5,4},{6,7},{7,6},{8,9},{9,8},{10,11... | collective-permute-start | bytes 663560 | tf_op jit(solution)/shard_map/ppermute | solution.py:367
  14.9 10.9 %collective-permute-start = (f32[3,36,512]{2,1,0:T(8,128)S(1)}, f32[3,36,512]{2,1,0:T(8,128)S(1)}, u32[]{:S(2)}, u32[]{:S(2)}) collective-permute-start(f32[3,36,512]{2,1,0:T(8,128)S(1)} %get-tuple-element.24), channel_id=1, source_target_pairs={{1,2},{2,1},{5,6},{6,5},{9,10},{10,9},{13,14},{14,13},{17,18},{18,... | collective-permute-start | bytes 663560 | tf_op jit(solution)/shard_map/ppermute | solution.py:368
  27.4 18.4 %all-to-all-start.1 = ((f32[32,8,384]{2,1,0:T(8,128)}), f32[32,8,384]{2,1,0:T(8,128)S(1)}, u32[]{:S(2)}, u32[]{:S(2)}) async-start(f32[32,8,384]{2,1,0:T(8,128)} %bitcast.6), calls=%async_computation.1 | async-start | bytes 786432 | tf_op jit(solution)/shard_map/all_to_all | solution.py:350

commit v6 on v5

--- a/solution.py
+++ b/solution.py
@@ -102,7 +102,7 @@
     slots = jnp.concatenate([send.astype(jnp.float32)] * N_MESH, axis=0)
     counts = jnp.broadcast_to(count.astype(jnp.float32), slots.shape)
     row = lax.broadcasted_iota(jnp.int32, slots.shape, 0)
-    mine = lax.broadcasted_iota(jnp.int32, slots.shape, 1) == row // CAP
+    mine = lax.broadcasted_iota(jnp.int32, slots.shape, 1) == N_MESH - 1 - row // CAP
     node = jnp.sum(jnp.where(mine, slots, 0.0), axis=1, keepdims=True)
     used = jnp.sum(jnp.where(mine, counts, 0.0), axis=1, keepdims=True)
     place = lax.broadcasted_iota(jnp.int32, (GHOSTS, 1), 0) % CAP
@@ -111,12 +111,9 @@
 
 
 def pack(hot, rows, packed_ref):
-    high = rows.astype(jnp.bfloat16)
-    low = (rows - high.astype(jnp.float32)).astype(jnp.bfloat16)
     dims = (((1,), (1,)), ((), ()))
-    packed_ref[:, :ROWS] = lax.dot_general(hot, high, dims, preferred_element_type=jnp.float32) + lax.dot_general(
-        hot, low, dims, preferred_element_type=jnp.float32
-    )
+    got = lax.dot_general(bf16_pieces(rows), hot, dims, preferred_element_type=jnp.float32)
+    packed_ref[:, :ROWS] = (got[:ROWS] + got[ROWS:]).T
     packed_ref[:, ROWS:] = jnp.zeros((GHOSTS, LANES - ROWS), jnp.float32)
 
 
@@ -188,6 +185,9 @@
     pack(hot_ref[...], rows_ref[...], packed_ref)
     for copy in copies[4:]:
         copy.wait()
+    entry = near_ref[...]
+    place = lax.rem(entry, CAP)
+    near_ref[...] = jnp.where(entry < NP, entry, NP + (NP + GHOSTS - CAP) - (entry - place) + place)
 
 
 def source(f, band, spectra_ref, lower_ref, upper_ref, along, base_ref):
@@ -347,7 +347,9 @@
 
     def exchange(packed):
         packed = packed.reshape(N_MESH, CAP, LANES)
-        return lax.all_to_all(packed, "mesh", split_axis=0, concat_axis=0, tiled=True).reshape(GHOSTS, LANES)
+        return lax.all_to_all(
+            packed, "mesh", split_axis=0, concat_axis=0, tiled=True, axis_index_groups=[list(range(N_MESH))[::-1]]
+        ).reshape(GHOSTS, LANES)
 
     def inside(*arrays):
         return [(array, VMEM) for array in arrays]

time: 48.8 us -> 44.5 us (0.912)
  waiting for transfers between devices: 11.2 us -> 2.65 us
  starting transfers between devices: 21.8 us -> 25.7 us
    all_to_all x2, waiting for transfers between devices: 11.2 us -> 2.64 us  [exchange(): lax.all_to_all(packed, 'mesh', split_axis=0, concat_axis=0, tiled=True, a...]
    all_to_all x2, starting transfers between devices: 18.6 us -> 22.4 us  [exchange(): lax.all_to_all(packed, 'mesh', split_axis=0, concat_axis=0, tiled=True, a...]
  transfers between devices with their start and end apart: 4 -> 4, of which waited for: 2 -> 1; matrix products, arithmetic and copies ran while one was open for 0% -> 0% of each run, Pallas kernels for 18% -> 20%
where the time goes in v6:
time: 44.5 us; the launch traced here: 43.7 us
  starting transfers between devices  25.7 us (58%)
  Pallas kernels  15.2 us (34%)
  waiting for transfers between devices  2.65 us (6%)
    all_to_all x2, starting transfers between devices, exchange(): lax.all_to_all(packed, 'mesh', split_axis=0, concat_axis=0, tiled=True, a...  22.4 us
    pallas_call x6, Pallas kernels, call(): pl.pallas_call(kernel, out_shape=[jax.ShapeDtypeStruct(shape, dtype) for...  15.2 us
    all_to_all x2, waiting for transfers between devices, exchange(): lax.all_to_all(packed, 'mesh', split_axis=0, concat_axis=0, tiled=True, a...  2.64 us
    ppermute x1, starting transfers between devices, local(): far_edge = lax.ppermute(far_edge, 'freq', pairs[1])  2.2 us
    ppermute x1, starting transfers between devices, local(): near_edge = lax.ppermute(near_edge, 'freq', pairs[0])  1.03 us
  transfers between devices with their start and end apart: 4, of which 1 were waited for; matrix products, arithmetic and copies ran while one was open for 0% of the time, Pallas kernels for 20%

profile of v6, /device:TPU:1, one launch (start us, length us, event | category | flops | bytes accessed | tf_op | source)
XLA Modules:
  0.0 43.7 jit_solution(13526396270742579399)
XLA Ops:
  0.0 2.5 %pack.1 = (f32[256,384]{1,0:T(8,128)}, f32[9,36,512]{2,1,0:T(8,128)S(1)}, f32[2,512]{1,0:T(2,128)S(1)}, s32[8,32]{1,0:T(8,128)S(1)}, s32[1,32]{1,0:T(1,128)S(1)}...) custom-call(s32[1]{0:T(128)} %bitcast.band_ref, ...), custom_call_target="tpu_custom_call" | custom-call | tf_op jit(solution)/shard_map/pack/pallas_call | solution.py:330
  2.5 13.2 %all-to-all-start = ((f32[32,8,384]{2,1,0:T(8,128)}), f32[32,8,384]{2,1,0:T(8,128)S(1)}, u32[]{:S(2)}, u32[]{:S(2)}) async-start(f32[32,8,384]{2,1,0:T(8,128)} %bitcast.4), calls=%async_computation | async-start | bytes 786432 | tf_op jit(solution)/shard_map/all_to_all | solution.py:350
  15.6 1.0 %collective-permute-start.1 = (f32[3,36,512]{2,1,0:T(8,128)S(1)}, f32[3,36,512]{2,1,0:T(8,128)S(1)}, u32[]{:S(2)}, u32[]{:S(2)}) collective-permute-start(f32[3,36,512]{2,1,0:T(8,128)S(1)} %get-tuple-element.26), channel_id=1, source_target_pairs={{0,1},{1,0},{2,3},{3,2},{4,5},{5,4},{6,7},{7,6},{8,9},{9,8},{10,11... | collective-permute-start | bytes 663560 | tf_op jit(solution)/shard_map/ppermute | solution.py:369
  16.7 2.2 %collective-permute-start = (f32[3,36,512]{2,1,0:T(8,128)S(1)}, f32[3,36,512]{2,1,0:T(8,128)S(1)}, u32[]{:S(2)}, u32[]{:S(2)}) collective-permute-start(f32[3,36,512]{2,1,0:T(8,128)S(1)} %get-tuple-element.24), channel_id=1, source_target_pairs={{1,2},{2,1},{5,6},{6,5},{9,10},{10,9},{13,14},{14,13},{17,18},{18,... | collective-permute-start | bytes 663560 | tf_op jit(solution)/shard_map/ppermute | solution.py:370
  18.9 0.0 collective-permute-done.1.near_edge_ref
  18.9 3.7 %local_first.1 = (f32[328,512]{1,0:T(8,128)S(1)}, f32[352,512]{1,0:T(8,128)S(1)}) custom-call(s32[1]{0:T(128)} %bitcast.band_ref, f32[9,36,512]{2,1,0:T(8,128)S(1)} %get-tuple-element.23.spectra_ref, f32[3,36,512]{2,1,0:T(8,128)S(1)} %collective-permute-done.1.near_edge_ref, f32[2,512]{1,0:T(2,128)S(1)} %get-tuple-element.27.coords_ref, ...), custom_call_target="tpu_custom_call" | custom-call | tf_op jit(solution)/shard_map/local_first/pallas_call | solution.py:330
  22.7 0.0 all-to-all-done
  22.7 1.8 %first_gather.1 = (f32[328,512]{1,0:T(8,128)S(1)}, f32[72,512]{1,0:T(8,128)S(1)}, f32[24,512]{1,0:T(8,128)S(1)}) custom-call(f32[256,384]{1,0:T(8,128)S(1)} %bitcast.8, f32[352,512]{1,0:T(8,128)S(1)} %get-tuple-element.32.partial_ref, f32[2,512]{1,0:T(2,128)S(1)} %get-tuple-element.27.coords_ref, s32[8,512]{1,0:T(8,128)S(1)} %get-tuple-element.29.near_ref), custom_call_target="tpu_custom_call" | custom-call | tf_op jit(solution)/shard_map/first_gather/pallas_call | solution.py:330
  24.4 0.0 collective-permute-done.far_edge_ref
  24.5 1.6 %first_settle.1 = (f32[256,384]{1,0:T(8,128)}, f32[328,512]{1,0:T(8,128)S(1)}, f32[328,512]{1,0:T(8,128)S(1)}) custom-call(s32[1]{0:T(128)} %bitcast.band_ref, f32[9,36,512]{2,1,0:T(8,128)S(1)} %get-tuple-element.23.spectra_ref, f32[3,36,512]{2,1,0:T(8,128)S(1)} %collective-permute-done.far_edge_ref, f32[2,512]{1,0:T(2,128)S(1)} %get-tuple-element.25.wind_ref, ...), custom_call_target="tpu_custom_call" | custom-call | tf_op jit(solution)/shard_map/first_settle/pallas_call | solution.py:330
  26.0 9.2 %all-to-all-start.1 = ((f32[32,8,384]{2,1,0:T(8,128)}), f32[32,8,384]{2,1,0:T(8,128)S(1)}, u32[]{:S(2)}, u32[]{:S(2)}) async-start(f32[32,8,384]{2,1,0:T(8,128)} %bitcast.6), calls=%async_computation.1 | async-start | bytes 786432 | tf_op jit(solution)/shard_map/all_to_all | solution.py:350
  35.3 3.1 %local_second.1.partial_ref = f32[328,512]{1,0:T(8,128)S(1)} custom-call(f32[328,512]{1,0:T(8,128)S(1)} %get-tuple-element.40.current_ref, f32[24,512]{1,0:T(8,128)S(1)} %get-tuple-element.35.delta_ref, s32[8,512]{1,0:T(8,128)S(1)} %get-tuple-element.29.near_ref), custom_call_target="tpu_custom_call" | custom-call | tf_op jit(solution)/shard_map/local_second/pallas_call | solution.py:330
  38.4 2.6 %all-to-all-done.1 = f32[32,8,384]{2,1,0:T(8,128)S(1)} async-done(((f32[32,8,384]{2,1,0:T(8,128)}), f32[32,8,384]{2,1,0:T(8,128)S(1)}, u32[]{:S(2)}, u32[]{:S(2)}) %all-to-all-start.1) | async-done | bytes 393248 | tf_op jit(solution)/shard_map/all_to_all | solution.py:350
  41.0 2.5 %second.1 = f32[9,36,512]{2,1,0:T(8,128)} custom-call(s32[1]{0:T(128)} %bitcast.band_ref, f32[256,384]{1,0:T(8,128)S(1)} %bitcast.9, f32[328,512]{1,0:T(8,128)S(1)} %get-tuple-element.39.base_ref, f32[328,512]{1,0:T(8,128)S(1)} %local_second.1.partial_ref, f32[24,512]{1,0:T(8,128)S(1)} %get-tuple-element.35.delta_ref, s32[8,512]{1,0:T(8,128)S(1)} %get-tuple-element.29.near_ref), custom_call_target="tpu_custom_call" | custom-call | tf_op jit(solution)/shard_map/second/pallas_call | solution.py:330
Async XLA Ops:
  2.5 20.2 %all-to-all-start = ((f32[32,8,384]{2,1,0:T(8,128)}), f32[32,8,384]{2,1,0:T(8,128)S(1)}, u32[]{:S(2)}, u32[]{:S(2)}) async-start(f32[32,8,384]{2,1,0:T(8,128)} %bitcast.4), calls=%async_computation | async-start | bytes 786432 | tf_op jit(solution)/shard_map/all_to_all | solution.py:350
  15.6 3.2 %collective-permute-start.1 = (f32[3,36,512]{2,1,0:T(8,128)S(1)}, f32[3,36,512]{2,1,0:T(8,128)S(1)}, u32[]{:S(2)}, u32[]{:S(2)}) collective-permute-start(f32[3,36,512]{2,1,0:T(8,128)S(1)} %get-tuple-element.26), channel_id=1, source_target_pairs={{0,1},{1,0},{2,3},{3,2},{4,5},{5,4},{6,7},{7,6},{8,9},{9,8},{10,11... | collective-permute-start | bytes 663560 | tf_op jit(solution)/shard_map/ppermute | solution.py:369
  16.7 7.8 %collective-permute-start = (f32[3,36,512]{2,1,0:T(8,128)S(1)}, f32[3,36,512]{2,1,0:T(8,128)S(1)}, u32[]{:S(2)}, u32[]{:S(2)}) collective-permute-start(f32[3,36,512]{2,1,0:T(8,128)S(1)} %get-tuple-element.24), channel_id=1, source_target_pairs={{1,2},{2,1},{5,6},{6,5},{9,10},{10,9},{13,14},{14,13},{17,18},{18,... | collective-permute-start | bytes 663560 | tf_op jit(solution)/shard_map/ppermute | solution.py:370
  26.0 15.0 %all-to-all-start.1 = ((f32[32,8,384]{2,1,0:T(8,128)}), f32[32,8,384]{2,1,0:T(8,128)S(1)}, u32[]{:S(2)}, u32[]{:S(2)}) async-start(f32[32,8,384]{2,1,0:T(8,128)} %bitcast.6), calls=%async_computation.1 | async-start | bytes 786432 | tf_op jit(solution)/shard_map/all_to_all | solution.py:350

commit v7 on v6

--- a/solution.py
+++ b/solution.py
@@ -102,7 +102,7 @@
     slots = jnp.concatenate([send.astype(jnp.float32)] * N_MESH, axis=0)
     counts = jnp.broadcast_to(count.astype(jnp.float32), slots.shape)
     row = lax.broadcasted_iota(jnp.int32, slots.shape, 0)
-    mine = lax.broadcasted_iota(jnp.int32, slots.shape, 1) == N_MESH - 1 - row // CAP
+    mine = lax.broadcasted_iota(jnp.int32, slots.shape, 1) == jnp.bitwise_xor(row // CAP, 22)
     node = jnp.sum(jnp.where(mine, slots, 0.0), axis=1, keepdims=True)
     used = jnp.sum(jnp.where(mine, counts, 0.0), axis=1, keepdims=True)
     place = lax.broadcasted_iota(jnp.int32, (GHOSTS, 1), 0) % CAP
@@ -186,8 +186,7 @@
     for copy in copies[4:]:
         copy.wait()
     entry = near_ref[...]
-    place = lax.rem(entry, CAP)
-    near_ref[...] = jnp.where(entry < NP, entry, NP + (NP + GHOSTS - CAP) - (entry - place) + place)
+    near_ref[...] = jnp.where(entry < NP, entry, NP + jnp.bitwise_xor(entry - NP, 22 * CAP))
 
 
 def source(f, band, spectra_ref, lower_ref, upper_ref, along, base_ref):
@@ -226,8 +225,6 @@
     cosine, sine = directions()
     along = cosine[:ND] * wind_ref[0:1, :] + sine[:ND] * wind_ref[1:2, :]
     base_ref[COORDS:] = jnp.zeros((ROWS - COORDS, NP), jnp.float32)
-    for f in range(DOWN_REACH, BAND - UP_REACH):
-        source(f, band, spectra_ref, None, None, along, base_ref)
     for k in range(K):
         entry = near_ref[k : k + 1, :]
         place, got = gather(pieces, entry, 0)
@@ -280,6 +277,8 @@
     cosine, sine = directions()
     along = cosine[:ND] * wind_ref[0:1, :] + sine[:ND] * wind_ref[1:2, :]
     base_ref[...] = part_ref[...]
+    for f in range(DOWN_REACH, BAND - UP_REACH):
+        source(f, band, spectra_ref, None, None, along, base_ref)
     edge_sources(lax.rem(band, 2) == 0, far_edge_ref, band, spectra_ref, along, base_ref)
     area, weight = delta_ref[2 * K : 2 * K + 1], weight_ref[...]
     for group in GROUPS:
@@ -348,7 +347,7 @@
     def exchange(packed):
         packed = packed.reshape(N_MESH, CAP, LANES)
         return lax.all_to_all(
-            packed, "mesh", split_axis=0, concat_axis=0, tiled=True, axis_index_groups=[list(range(N_MESH))[::-1]]
+            packed, "mesh", split_axis=0, concat_axis=0, tiled=True, axis_index_groups=[[i ^ 22 for i in range(N_MESH)]]
         ).reshape(GHOSTS, LANES)
 
     def inside(*arrays):

time: 44.5 us -> 44.1 us (level)
  waiting for transfers between devices: 2.65 us -> 1.88 us
  starting transfers between devices: 25.7 us -> 26.4 us
    all_to_all x2, waiting for transfers between devices: 2.64 us -> 1.87 us  [exchange(): lax.all_to_all(packed, 'mesh', split_axis=0, concat_axis=0, tiled=True, a...]
    ppermute x1, starting transfers between devices: 2.2 us -> 2.88 us  [local(): far_edge = lax.ppermute(far_edge, 'freq', pairs[1])]
  transfers between devices with their start and end apart: 4 -> 4, of which waited for: 1 -> 1; matrix products, arithmetic and copies ran while one was open for 0% -> 0% of each run, Pallas kernels for 20% -> 19%
where the time goes in v7:
time: 44.1 us; the launch traced here: 43.7 us
  starting transfers between devices  26.4 us (60%)
  Pallas kernels  15.2 us (34%)
  waiting for transfers between devices  1.88 us (4%)
    all_to_all x2, starting transfers between devices, exchange(): lax.all_to_all(packed, 'mesh', split_axis=0, concat_axis=0, tiled=True, a...  22.5 us
    pallas_call x6, Pallas kernels, call(): pl.pallas_call(kernel, out_shape=[jax.ShapeDtypeStruct(shape, dtype) for...  15.2 us
    ppermute x1, starting transfers between devices, local(): far_edge = lax.ppermute(far_edge, 'freq', pairs[1])  2.88 us
    all_to_all x2, waiting for transfers between devices, exchange(): lax.all_to_all(packed, 'mesh', split_axis=0, concat_axis=0, tiled=True, a...  1.87 us
    ppermute x1, starting transfers between devices, local(): near_edge = lax.ppermute(near_edge, 'freq', pairs[0])  1.08 us
  transfers between devices with their start and end apart: 4, of which 1 were waited for; matrix products, arithmetic and copies ran while one was open for 0% of the time, Pallas kernels for 19%

profile of v7, /device:TPU:1, one launch (start us, length us, event | category | flops | bytes accessed | tf_op | source)
XLA Modules:
  0.0 43.7 jit_solution(290707823042010952)
XLA Ops:
  0.0 2.5 %pack.1 = (f32[256,384]{1,0:T(8,128)}, f32[9,36,512]{2,1,0:T(8,128)S(1)}, f32[2,512]{1,0:T(2,128)S(1)}, s32[8,32]{1,0:T(8,128)S(1)}, s32[1,32]{1,0:T(1,128)S(1)}...) custom-call(s32[1]{0:T(128)} %bitcast.band_ref, ...), custom_call_target="tpu_custom_call" | custom-call | tf_op jit(solution)/shard_map/pack/pallas_call | solution.py:329
  2.5 13.2 %all-to-all-start = ((f32[32,8,384]{2,1,0:T(8,128)}), f32[32,8,384]{2,1,0:T(8,128)S(1)}, u32[]{:S(2)}, u32[]{:S(2)}) async-start(f32[32,8,384]{2,1,0:T(8,128)} %bitcast.4), calls=%async_computation | async-start | bytes 786432 | tf_op jit(solution)/shard_map/all_to_all | solution.py:349
  15.7 1.1 %collective-permute-start.1 = (f32[3,36,512]{2,1,0:T(8,128)S(1)}, f32[3,36,512]{2,1,0:T(8,128)S(1)}, u32[]{:S(2)}, u32[]{:S(2)}) collective-permute-start(f32[3,36,512]{2,1,0:T(8,128)S(1)} %get-tuple-element.26), channel_id=1, source_target_pairs={{0,1},{1,0},{2,3},{3,2},{4,5},{5,4},{6,7},{7,6},{8,9},{9,8},{10,11... | collective-permute-start | bytes 663560 | tf_op jit(solution)/shard_map/ppermute | solution.py:368
  16.8 2.9 %collective-permute-start = (f32[3,36,512]{2,1,0:T(8,128)S(1)}, f32[3,36,512]{2,1,0:T(8,128)S(1)}, u32[]{:S(2)}, u32[]{:S(2)}) collective-permute-start(f32[3,36,512]{2,1,0:T(8,128)S(1)} %get-tuple-element.24), channel_id=1, source_target_pairs={{1,2},{2,1},{5,6},{6,5},{9,10},{10,9},{13,14},{14,13},{17,18},{18,... | collective-permute-start | bytes 663560 | tf_op jit(solution)/shard_map/ppermute | solution.py:369
  19.7 0.0 collective-permute-done.1.near_edge_ref
  19.7 3.4 %local_first.1 = (f32[328,512]{1,0:T(8,128)S(1)}, f32[352,512]{1,0:T(8,128)S(1)}) custom-call(s32[1]{0:T(128)} %bitcast.band_ref, f32[9,36,512]{2,1,0:T(8,128)S(1)} %get-tuple-element.23.spectra_ref, f32[3,36,512]{2,1,0:T(8,128)S(1)} %collective-permute-done.1.near_edge_ref, f32[2,512]{1,0:T(2,128)S(1)} %get-tuple-element.27.coords_ref, ...), custom_call_target="tpu_custom_call" | custom-call | tf_op jit(solution)/shard_map/local_first/pallas_call | solution.py:329
  23.1 0.0 all-to-all-done
  23.1 1.8 %first_gather.1 = (f32[328,512]{1,0:T(8,128)S(1)}, f32[72,512]{1,0:T(8,128)S(1)}, f32[24,512]{1,0:T(8,128)S(1)}) custom-call(f32[256,384]{1,0:T(8,128)S(1)} %bitcast.8, f32[352,512]{1,0:T(8,128)S(1)} %get-tuple-element.32.partial_ref, f32[2,512]{1,0:T(2,128)S(1)} %get-tuple-element.27.coords_ref, s32[8,512]{1,0:T(8,128)S(1)} %get-tuple-element.29.near_ref), custom_call_target="tpu_custom_call" | custom-call | tf_op jit(solution)/shard_map/first_gather/pallas_call | solution.py:329
  24.8 0.0 collective-permute-done.far_edge_ref
  24.9 1.9 %first_settle.1 = (f32[256,384]{1,0:T(8,128)}, f32[328,512]{1,0:T(8,128)S(1)}, f32[328,512]{1,0:T(8,128)S(1)}) custom-call(s32[1]{0:T(128)} %bitcast.band_ref, f32[9,36,512]{2,1,0:T(8,128)S(1)} %get-tuple-element.23.spectra_ref, f32[3,36,512]{2,1,0:T(8,128)S(1)} %collective-permute-done.far_edge_ref, f32[2,512]{1,0:T(2,128)S(1)} %get-tuple-element.25.wind_ref, ...), custom_call_target="tpu_custom_call" | custom-call | tf_op jit(solution)/shard_map/first_settle/pallas_call | solution.py:329
  26.8 9.2 %all-to-all-start.1 = ((f32[32,8,384]{2,1,0:T(8,128)}), f32[32,8,384]{2,1,0:T(8,128)S(1)}, u32[]{:S(2)}, u32[]{:S(2)}) async-start(f32[32,8,384]{2,1,0:T(8,128)} %bitcast.6), calls=%async_computation.1 | async-start | bytes 786432 | tf_op jit(solution)/shard_map/all_to_all | solution.py:349
  36.0 3.1 %local_second.1.partial_ref = f32[328,512]{1,0:T(8,128)S(1)} custom-call(f32[328,512]{1,0:T(8,128)S(1)} %get-tuple-element.40.current_ref, f32[24,512]{1,0:T(8,128)S(1)} %get-tuple-element.35.delta_ref, s32[8,512]{1,0:T(8,128)S(1)} %get-tuple-element.29.near_ref), custom_call_target="tpu_custom_call" | custom-call | tf_op jit(solution)/shard_map/local_second/pallas_call | solution.py:329
  39.1 1.9 %all-to-all-done.1 = f32[32,8,384]{2,1,0:T(8,128)S(1)} async-done(((f32[32,8,384]{2,1,0:T(8,128)}), f32[32,8,384]{2,1,0:T(8,128)S(1)}, u32[]{:S(2)}, u32[]{:S(2)}) %all-to-all-start.1) | async-done | bytes 393248 | tf_op jit(solution)/shard_map/all_to_all | solution.py:349
  41.0 2.5 %second.1 = f32[9,36,512]{2,1,0:T(8,128)} custom-call(s32[1]{0:T(128)} %bitcast.band_ref, f32[256,384]{1,0:T(8,128)S(1)} %bitcast.9, f32[328,512]{1,0:T(8,128)S(1)} %get-tuple-element.39.base_ref, f32[328,512]{1,0:T(8,128)S(1)} %local_second.1.partial_ref, f32[24,512]{1,0:T(8,128)S(1)} %get-tuple-element.35.delta_ref, s32[8,512]{1,0:T(8,128)S(1)} %get-tuple-element.29.near_ref), custom_call_target="tpu_custom_call" | custom-call | tf_op jit(solution)/shard_map/second/pallas_call | solution.py:329
Async XLA Ops:
  2.5 20.6 %all-to-all-start = ((f32[32,8,384]{2,1,0:T(8,128)}), f32[32,8,384]{2,1,0:T(8,128)S(1)}, u32[]{:S(2)}, u32[]{:S(2)}) async-start(f32[32,8,384]{2,1,0:T(8,128)} %bitcast.4), calls=%async_computation | async-start | bytes 786432 | tf_op jit(solution)/shard_map/all_to_all | solution.py:349
  15.7 4.0 %collective-permute-start.1 = (f32[3,36,512]{2,1,0:T(8,128)S(1)}, f32[3,36,512]{2,1,0:T(8,128)S(1)}, u32[]{:S(2)}, u32[]{:S(2)}) collective-permute-start(f32[3,36,512]{2,1,0:T(8,128)S(1)} %get-tuple-element.26), channel_id=1, source_target_pairs={{0,1},{1,0},{2,3},{3,2},{4,5},{5,4},{6,7},{7,6},{8,9},{9,8},{10,11... | collective-permute-start | bytes 663560 | tf_op jit(solution)/shard_map/ppermute | solution.py:368
  16.8 8.1 %collective-permute-start = (f32[3,36,512]{2,1,0:T(8,128)S(1)}, f32[3,36,512]{2,1,0:T(8,128)S(1)}, u32[]{:S(2)}, u32[]{:S(2)}) collective-permute-start(f32[3,36,512]{2,1,0:T(8,128)S(1)} %get-tuple-element.24), channel_id=1, source_target_pairs={{1,2},{2,1},{5,6},{6,5},{9,10},{10,9},{13,14},{14,13},{17,18},{18,... | collective-permute-start | bytes 663560 | tf_op jit(solution)/shard_map/ppermute | solution.py:369
  26.8 14.2 %all-to-all-start.1 = ((f32[32,8,384]{2,1,0:T(8,128)}), f32[32,8,384]{2,1,0:T(8,128)S(1)}, u32[]{:S(2)}, u32[]{:S(2)}) async-start(f32[32,8,384]{2,1,0:T(8,128)} %bitcast.6), calls=%async_computation.1 | async-start | bytes 786432 | tf_op jit(solution)/shard_map/all_to_all | solution.py:349
